TPU v7x, 32 devices: a whole 2x2x4 slice. The times are simulated.
32 devices in a mesh: dp: 8 (over z, x), seq: 4 (over y, core).
Axes of the slice: x: 2, y: 2, z: 4, core: 2. Of those that a mesh axis runs over, the one named last changes fastest.
Arguments:
- tokens: bfloat16 [2, 16384, 768], P(None, ('dp', 'seq')), may hold values from -6 to 6
- cotangent: bfloat16 [2, 16384, 768], P(None, ('dp', 'seq')), may hold values from -6 to 6
- lengths: int32 [2, 8, 4], P(None, 'dp'), may hold values from 1 to 1365, 2048 in all within a row
- gain_first: bfloat16 [768], P(('dp', 'seq')), may hold values from 0.5 to 1.5
- shift_first: bfloat16 [768], P(('dp', 'seq')), may hold values from -3 to 3
- packed_weight: bfloat16 [768, 2304], P(('dp', 'seq')), may hold values from -0.21875 to 0.21875
- packed_bias: bfloat16 [1536], P(('dp', 'seq')), may hold values from -3 to 3
- output_weight: bfloat16 [768, 768], P(('dp', 'seq')), may hold values from -6 to 6
- output_bias: bfloat16 [768], P(('dp', 'seq')), may hold values from -3 to 3
- gain_second: bfloat16 [768], P(('dp', 'seq')), may hold values from 0.5 to 1.5
- shift_second: bfloat16 [768], P(('dp', 'seq')), may hold values from -3 to 3
- expand_weight: bfloat16 [768, 3072], P(('dp', 'seq')), may hold values from -0.21875 to 0.21875
- expand_bias: bfloat16 [3072], P(('dp', 'seq')), may hold values from -3 to 3
- reduce_weight: bfloat16 [3072, 768], P(('dp', 'seq')), may hold values from -0.375 to 0.375
- reduce_bias: bfloat16 [768], P(('dp', 'seq')), may hold values from -3 to 3
Outputs:
- layer_output: bfloat16 [2, 16384, 768], P(None, ('dp', 'seq'))
- input_grad: bfloat16 [2, 16384, 768], P(None, ('dp', 'seq'))
- gain_first_grad: float32 [768], P(('dp', 'seq'))
- shift_first_grad: float32 [768], P(('dp', 'seq'))
- packed_weight_grad: float32 [768, 2304], P(('dp', 'seq'))
- packed_bias_grad: float32 [1536], P(('dp', 'seq'))
- output_weight_grad: float32 [768, 768], P(('dp', 'seq'))
- output_bias_grad: float32 [768], P(('dp', 'seq'))
- gain_second_grad: float32 [768], P(('dp', 'seq'))
- shift_second_grad: float32 [768], P(('dp', 'seq'))
- expand_weight_grad: float32 [768, 3072], P(('dp', 'seq'))
- expand_bias_grad: float32 [3072], P(('dp', 'seq'))
- reduce_weight_grad: float32 [3072, 768], P(('dp', 'seq'))
- reduce_bias_grad: float32 [768], P(('dp', 'seq'))
Inputs may be any that keep to these rules, and one draw needn't show every extreme that they name: Each row lengths[m, g] has 3 sequence lengths in order, then the padding length; it sums to 2048 and its largest entry is exactly 1365. Every entry, sequences and padding alike, lies anywhere from 1 to 1365; there is no larger lower bound. The padding mask is not an argument: it follows from the lengths.
All inputs are finite; a program needn't handle non-finite values.
Results may differ from a plain program's by a relative error of at most 0.011.
Values may be sent and summed in bfloat16 or wider, within the bound.
A program may use at most 192 MiB of HBM per device.

v0:
```python
import functools

import jax
import jax.numpy as jnp
from jax import lax
from jax.experimental import pallas as pl
from jax.experimental.pallas import tpu as pltpu
from jax.sharding import PartitionSpec as P

H = 12
HD = 64
BRANCH_SCALE = 12 ** (-0.5)
EPSILON = 1e-05
F32 = jnp.float32
BF16 = jnp.bfloat16
TILE = 256
PAIR = 2 * HD
MASKED = -1e30


def outer_sum(first, second):
    return lax.dot_general(first, second, (((0,), (0,)), ((), ())), preferred_element_type=F32)


def against_rows(first, second):
    return lax.dot_general(first, second, (((1,), (1,)), ((), ())), preferred_element_type=F32)


def layer_norm(values, norm_gain, norm_shift):
    center = values - jnp.mean(values, axis=-1, keepdims=True)
    spread = jnp.mean(center * center, axis=-1, keepdims=True)
    return center * lax.rsqrt(spread + EPSILON) * norm_gain + norm_shift


def gelu_tanh(values):
    return jax.nn.gelu(values, approximate=True)


def split_pair(rows):
    lane = lax.broadcasted_iota(jnp.int32, rows.shape, 1)
    nothing = jnp.zeros_like(rows)
    return jnp.where(lane < HD, rows, nothing), jnp.where(lane < HD, nothing, rows)


def allowed_in(key_block, row_block, begins, diagonal):
    keys = key_block * TILE + lax.broadcasted_iota(jnp.int32, (TILE, TILE), 0)
    allowed = keys >= begins
    if diagonal:
        rows = row_block * TILE + lax.broadcasted_iota(jnp.int32, (TILE, TILE), 1)
        allowed = allowed & (keys <= rows)
    return allowed


def attend_kernel(low_ref, q_ref, k_ref, v_ref, begin_ref, out_ref, logsum_ref, value_t):
    blocks = q_ref.shape[0] // TILE
    for block in range(blocks):
        at = slice(block * TILE, (block + 1) * TILE)
        value_t[:, at] = v_ref[at, :].T

    def one_row_block(i, carry):
        here = pl.ds(pl.multiple_of(i * TILE, TILE), TILE)
        heads = split_pair(q_ref[here, :] * HD ** (-0.5))
        begins = begin_ref[:, here]

        def visit(j, state, diagonal):
            there = pl.ds(pl.multiple_of(j * TILE, TILE), TILE)
            key_rows = k_ref[there, :]
            allowed = allowed_in(j, i, begins, diagonal)
            new_state = []
            for which in range(2):
                scores = against_rows(key_rows, heads[which])
                scores = jnp.where(allowed, scores, MASKED)
                top = jnp.max(scores, axis=0, keepdims=True)
                if state is not None:
                    old_top, old_total, old_mix = state[which]
                    top = jnp.maximum(top, old_top)
                weights = jnp.exp(scores - top)
                total = jnp.sum(weights, axis=0, keepdims=True)
                mix = jnp.dot(
                    value_t[which * HD : (which + 1) * HD, there],
                    weights.astype(BF16),
                    preferred_element_type=F32,
                )
                if state is not None:
                    fade = jnp.exp(old_top - top)
                    total = total + fade * old_total
                    mix = mix + fade * old_mix
                new_state.append((top, total, mix))
            return tuple(new_state)

        state = visit(i, None, True)
        state = lax.fori_loop(low_ref[i], i, lambda j, s: visit(j, s, False), state)
        mixed = [mix / total for _, total, mix in state]
        out_ref[here, :] = jnp.concatenate(mixed, axis=0).T.astype(BF16)
        logs = [top + jnp.log(total) for top, total, _ in state]
        logsum_ref[0, :, here] = jnp.concatenate(logs, axis=0)
        return carry

    lax.fori_loop(0, blocks, one_row_block, 0)


def attend_forward(packed, low_blocks, begins):
    bucket, columns = packed.shape
    groups = columns // 3 // PAIR
    tall = lambda first: pl.BlockSpec((bucket, PAIR), lambda g, low: (0, first + g))
    return pl.pallas_call(
        attend_kernel,
        name="attend_forward",
        out_shape=(
            jax.ShapeDtypeStruct((bucket, columns // 3), BF16),
            jax.ShapeDtypeStruct((groups, 2, bucket), F32),
        ),
        grid_spec=pltpu.PrefetchScalarGridSpec(
            num_scalar_prefetch=1,
            grid=(groups,),
            in_specs=[
                tall(0),
                tall(groups),
                tall(2 * groups),
                pl.BlockSpec((1, bucket), lambda g, low: (0, 0)),
            ],
            out_specs=[tall(0), pl.BlockSpec((1, 2, bucket), lambda g, low: (g, 0, 0))],
            scratch_shapes=[pltpu.VMEM((PAIR, bucket), BF16)],
        ),
        cost_estimate=pl.CostEstimate(
            flops=4 * 2 * groups * bucket * bucket * HD // 2,
            bytes_accessed=bucket * columns * 3,
            transcendentals=2 * groups * bucket * bucket // 2,
        ),
    )(low_blocks, packed, packed, packed, begins)


def attend_back_kernel(
    high_ref, q_ref, k_ref, v_ref, o_ref, go_ref, begin_ref, logsum_ref, out_ref, key_t, query_t, delta
):
    blocks = q_ref.shape[0] // TILE
    half = lax.broadcasted_iota(jnp.int32, (8, PAIR), 1) // HD
    picks = (half == lax.broadcasted_iota(jnp.int32, (8, PAIR), 0)).astype(F32)
    for block in range(blocks):
        at = slice(block * TILE, (block + 1) * TILE)
        key_t[:, at] = k_ref[at, :].T
        query_t[:, at] = jnp.zeros((PAIR, TILE), F32)
        product = o_ref[at, :].astype(F32) * go_ref[at, :].astype(F32)
        delta[:, at] = lax.dot_general(
            picks,
            product,
            (((1,), (1,)), ((), ())),
            precision=lax.Precision.HIGHEST,
            preferred_element_type=F32,
        )

    def one_key_block(j, carry):
        there = pl.ds(pl.multiple_of(j * TILE, TILE), TILE)
        key_rows = k_ref[there, :]
        value_rows = v_ref[there, :]

        def visit(i, state, diagonal):
            here = pl.ds(pl.multiple_of(i * TILE, TILE), TILE)
            queries = split_pair(q_ref[here, :] * HD ** (-0.5))
            grads = split_pair(go_ref[here, :])
            allowed = allowed_in(j, i, begin_ref[:, here], diagonal)
            key_grad, value_grad = state
            for which in range(2):
                scores = against_rows(key_rows, queries[which])
                scores = jnp.where(allowed, scores, MASKED)
                probs = jnp.exp(scores - logsum_ref[0, which : which + 1, here])
                grad_probs = against_rows(value_rows, grads[which])
                grad_scores = (probs * (grad_probs - delta[which : which + 1, here])).astype(BF16)
                value_grad = value_grad + jnp.dot(
                    probs.astype(BF16), grads[which], preferred_element_type=F32
                )
                key_grad = key_grad + jnp.dot(
                    grad_scores, queries[which], preferred_element_type=F32
                )
                at = slice(which * HD, (which + 1) * HD)
                query_t[at, here] += jnp.dot(
                    key_t[at, there], grad_scores, preferred_element_type=F32
                )
            return key_grad, value_grad

        zero = jnp.zeros((TILE, PAIR), F32)
        state = visit(j, (zero, zero), True)
        state = lax.fori_loop(j + 1, high_ref[j], lambda i, s: visit(i, s, False), state)
        out_ref[1, there, :] = state[0].astype(BF16)
        out_ref[2, there, :] = state[1].astype(BF16)
        return carry

    lax.fori_loop(0, blocks, one_key_block, 0)
    for block in range(blocks):
        at = slice(block * TILE, (block + 1) * TILE)
        out_ref[0, at, :] = (query_t[:, at].T * HD ** (-0.5)).astype(BF16)


def attend_backward(packed, attended, grad_attended, logsum, high_blocks, begins):
    bucket, columns = packed.shape
    groups = columns // 3 // PAIR
    tall = lambda first: pl.BlockSpec((bucket, PAIR), lambda g, high: (0, first + g))
    return pl.pallas_call(
        attend_back_kernel,
        name="attend_backward",
        out_shape=jax.ShapeDtypeStruct((3, bucket, columns // 3), BF16),
        grid_spec=pltpu.PrefetchScalarGridSpec(
            num_scalar_prefetch=1,
            grid=(groups,),
            in_specs=[
                tall(0),
                tall(groups),
                tall(2 * groups),
                tall(0),
                tall(0),
                pl.BlockSpec((1, bucket), lambda g, high: (0, 0)),
                pl.BlockSpec((1, 2, bucket), lambda g, high: (g, 0, 0)),
            ],
            out_specs=pl.BlockSpec((3, bucket, PAIR), lambda g, high: (0, 0, g)),
            scratch_shapes=[
                pltpu.VMEM((PAIR, bucket), BF16),
                pltpu.VMEM((PAIR, bucket), F32),
                pltpu.VMEM((8, bucket), F32),
            ],
        ),
        cost_estimate=pl.CostEstimate(
            flops=10 * 2 * groups * bucket * bucket * HD // 2,
            bytes_accessed=bucket * columns * 6,
            transcendentals=2 * groups * bucket * bucket // 2,
        ),
    )(high_blocks, packed, packed, packed, attended, grad_attended, begins, logsum)


def gather_rows(shard):
    return lax.all_gather(shard, ("dp", "seq"), axis=0, tiled=True)


def scatter_sum(full):
    return lax.psum_scatter(full, ("dp", "seq"), scatter_dimension=0, tiled=True)


def local(
    tokens,
    cotangent,
    lengths,
    gain_first,
    shift_first,
    packed_weight,
    packed_bias,
    output_weight,
    output_bias,
    gain_second,
    shift_second,
    expand_weight,
    expand_bias,
    reduce_weight,
    reduce_bias,
):
    micro_count, local_rows, width = tokens.shape
    groups = lax.axis_size("seq")
    devices = groups * lax.axis_size("dp")
    share = groups // micro_count
    bucket = local_rows * groups
    hidden_width = expand_weight.shape[1]
    columns = width // share
    place = lax.axis_index("seq")
    mine, core = place // share, place % share
    swap_micro = [(s, (s + share) % groups) for s in range(groups)]
    swap_core = [(s, s ^ 1) for s in range(groups)]

    def own_micro(both):
        kept = lax.dynamic_index_in_dim(both, mine, 0, keepdims=False)
        sent = lax.dynamic_index_in_dim(both, 1 - mine, 0, keepdims=False)
        came = lax.ppermute(sent, "seq", swap_micro)
        return jnp.stack([jnp.where(mine == 0, kept, came), jnp.where(mine == 0, came, kept)])

    def home_micro(blocks):
        kept = lax.dynamic_index_in_dim(blocks, mine, 0, keepdims=False)
        sent = lax.dynamic_index_in_dim(blocks, 1 - mine, 0, keepdims=False)
        came = lax.ppermute(sent, "seq", swap_micro)
        return jnp.stack([jnp.where(mine == 0, kept, came), jnp.where(mine == 0, came, kept)])

    def interleave(own, other):
        first, second = jnp.where(core == 0, own, other), jnp.where(core == 0, other, own)
        return jnp.stack([first, second], axis=1).reshape((bucket,) + own.shape[2:])

    own_tokens = own_micro(tokens)
    own_cotangent = own_micro(cotangent)
    other_tokens = lax.ppermute(own_tokens, "seq", swap_core)

    vectors = (gain_first, shift_first, packed_bias, output_bias, gain_second, shift_second, expand_bias, reduce_bias)
    sizes = [v.shape[0] for v in vectors]
    small_count = sum(sizes)
    pieces_per_row = hidden_width // width
    rows = output_weight.shape[0]
    extra = jnp.pad(jnp.concatenate(vectors), (0, 8 * 3 * width - small_count)).reshape(8, 3 * width)
    first = gather_rows(jnp.concatenate([packed_weight, extra])).reshape(devices, rows + 8, 3 * width)
    expand_blocks = [expand_weight[:, j * width : (j + 1) * width] for j in range(pieces_per_row)]
    second = gather_rows(jnp.concatenate([output_weight] + expand_blocks + [reduce_weight])).reshape(devices, -1, width)
    full_packed = first[:, :rows].reshape(width, 3 * width)
    small_all = first[:, rows]
    full_output = second[:, :rows].reshape(width, width)
    full_expand = jnp.concatenate(
        [second[:, rows * (j + 1) : rows * (j + 2)].reshape(width, width) for j in range(pieces_per_row)], axis=1
    )
    full_reduce = second[:, rows * (pieces_per_row + 1) :].reshape(hidden_width, width)
    pieces, at = [], 0
    for size in sizes:
        pieces.append(small_all[:, at : at + size].reshape(-1).astype(F32))
        at += size
    gain_one, shift_one, packed_shift, output_shift, gain_two, shift_two, expand_shift, reduce_shift = pieces

    places = jnp.arange(bucket, dtype=jnp.int32)
    bucket_lengths = lax.dynamic_index_in_dim(lengths, mine, 0, keepdims=False)[0]
    slot_count = lengths.shape[-1]
    ends = jnp.cumsum(bucket_lengths)
    past = (places[:, None] >= ends[None, :]).astype(jnp.int32)
    begins = jnp.sum(past * bucket_lengths[None, :], axis=1)
    low_blocks = begins[::TILE] // TILE
    block_ids = jnp.arange(bucket // TILE, dtype=jnp.int32)
    high_blocks = jnp.sum((low_blocks[None, :] <= block_ids[:, None]).astype(jnp.int32), axis=1)
    begins = begins[None, :]
    valid_all = (jnp.sum(past, axis=1) < slot_count - 1).astype(F32).reshape(2, share, local_rows)
    valid = lax.dynamic_index_in_dim(valid_all, core, 1, keepdims=False).reshape(-1, 1)

    inputs = own_tokens.reshape(-1, width).astype(F32)
    everyone = interleave(own_tokens, other_tokens).astype(F32)
    normed_low = layer_norm(everyone, gain_one, shift_one).astype(BF16)
    half_packed = jnp.concatenate(
        [lax.dynamic_slice(full_packed, (0, part * width + core * columns), (width, columns)) for part in range(3)], axis=1
    )
    bias_row = jnp.concatenate([packed_shift[:width], jnp.zeros((width,), F32), packed_shift[width:]])
    half_bias = jnp.concatenate(
        [lax.dynamic_slice(bias_row, (part * width + core * columns,), (columns,)) for part in range(3)]
    )
    packed = (jnp.dot(normed_low, half_packed, preferred_element_type=F32) + half_bias).astype(BF16)
    attended_heads, logsum = attend_forward(packed, low_blocks, begins)

    by_core = attended_heads.reshape(2, share, local_rows, columns)
    kept = lax.dynamic_index_in_dim(by_core, core, 1, keepdims=False)
    came = lax.ppermute(lax.dynamic_index_in_dim(by_core, 1 - core, 1, keepdims=False), "seq", swap_core)
    attended = jnp.concatenate(
        [jnp.where(core == 0, kept, came), jnp.where(core == 0, came, kept)], axis=-1
    ).reshape(-1, width)

    middle = inputs + BRANCH_SCALE * (
        jnp.dot(attended, full_output, preferred_element_type=F32) + output_shift
    )
    normed_two, norm_back_two = jax.vjp(layer_norm, middle, gain_two, shift_two)
    normed_two_low = normed_two.astype(BF16)
    activated, gelu_back = jax.vjp(
        gelu_tanh, jnp.dot(normed_two_low, full_expand, preferred_element_type=F32) + expand_shift
    )
    active_low = activated.astype(BF16)
    branch_out = jnp.dot(active_low, full_reduce, preferred_element_type=F32) + reduce_shift
    layer_rows = ((middle + BRANCH_SCALE * branch_out) * valid).astype(BF16)

    grad_rows = own_cotangent.reshape(-1, width).astype(F32) * valid
    grad_branch = (BRANCH_SCALE * grad_rows).astype(BF16)
    reduce_weight_grad = outer_sum(active_low, grad_branch)
    reduce_bias_grad = jnp.sum(grad_branch.astype(F32), axis=0)
    (grad_hidden,) = gelu_back(against_rows(grad_branch, full_reduce))
    grad_hidden = grad_hidden.astype(BF16)
    expand_weight_grad = outer_sum(normed_two_low, grad_hidden)
    expand_bias_grad = jnp.sum(grad_hidden.astype(F32), axis=0)
    middle_part, gain_two_grad, shift_two_grad = norm_back_two(against_rows(grad_hidden, full_expand))
    grad_middle = grad_rows + middle_part
    grad_proj = (BRANCH_SCALE * grad_middle).astype(BF16)
    output_weight_grad = outer_sum(attended, grad_proj)
    output_bias_grad = jnp.sum(grad_proj.astype(F32), axis=0)
    expand_grads = [
        expand_weight_grad[:, j * width : (j + 1) * width].astype(BF16).reshape(devices, rows, width)
        for j in range(pieces_per_row)
    ]
    early = jnp.concatenate(
        [output_weight_grad.astype(BF16).reshape(devices, rows, width)]
        + expand_grads
        + [reduce_weight_grad.astype(BF16).reshape(devices, -1, width)],
        axis=1,
    )
    early_sum = scatter_sum(early.reshape(-1, width)).astype(F32)
    grad_attended = against_rows(grad_proj, full_output).astype(BF16).reshape(2, local_rows, share, columns)
    kept = lax.dynamic_index_in_dim(grad_attended, core, 2, keepdims=False)
    came = lax.ppermute(
        lax.dynamic_index_in_dim(grad_attended, 1 - core, 2, keepdims=False), "seq", swap_core
    )
    grad_heads = interleave(kept, came)
    grad_packed = attend_backward(packed, attended_heads, grad_heads, logsum, high_blocks, begins)
    half_grads = [outer_sum(normed_low, grad_packed[part]).astype(BF16) for part in range(3)]
    half_sums = jnp.sum(grad_packed.astype(F32), axis=1)
    part_grad = sum(
        against_rows(grad_packed[part], half_packed[:, part * columns : (part + 1) * columns]) for part in range(3)
    ).astype(BF16)
    by_core = part_grad.reshape(2, share, local_rows, width)
    kept = lax.dynamic_index_in_dim(by_core, core, 1, keepdims=False)
    came = lax.ppermute(lax.dynamic_index_in_dim(by_core, 1 - core, 1, keepdims=False), "seq", swap_core)
    norm_grad = (kept.astype(F32) + came.astype(F32)).reshape(-1, width)
    _, norm_back_one = jax.vjp(layer_norm, inputs, gain_one, shift_one)
    input_part, gain_one_grad, shift_one_grad = norm_back_one(norm_grad)
    input_rows = (grad_middle + input_part).astype(BF16)

    layer_output = home_micro(layer_rows.reshape(2, local_rows, width))
    input_grad = home_micro(input_rows.reshape(2, local_rows, width))

    def spread(half):
        nothing = jnp.zeros_like(half)
        return [jnp.where(core == place_of, half, nothing) for place_of in range(share)]

    half_places = [block for half in half_grads for block in spread(half)]
    packed_bias_grad = jnp.concatenate([block for part in (0, 2) for block in spread(half_sums[part])])
    small_grads = [gain_one_grad, shift_one_grad, packed_bias_grad, output_bias_grad, gain_two_grad, shift_two_grad, expand_bias_grad, reduce_bias_grad]
    small_rows = jnp.concatenate([g.reshape(devices, -1) for g in small_grads], axis=1).astype(BF16)
    small_rows = jnp.pad(small_rows, ((0, 0), (0, 8 * 3 * width - small_count))).reshape(devices, 8, 3 * width)
    last = jnp.concatenate(
        [jnp.concatenate(half_places, axis=1).reshape(devices, rows, 3 * width), small_rows], axis=1
    )
    last_sum = scatter_sum(last.reshape(-1, 3 * width)).astype(F32)
    small_sum = last_sum[rows]
    pieces, at = [], 0
    for size in sizes:
        pieces.append(small_sum[at : at + size])
        at += size
    expand_sum = jnp.concatenate(
        [early_sum[rows * (j + 1) : rows * (j + 2)] for j in range(pieces_per_row)], axis=1
    )
    big = (early_sum[rows * (pieces_per_row + 1) :], expand_sum, early_sum[:rows], last_sum[:rows])
    return (
        layer_output,
        input_grad,
        pieces[0],
        pieces[1],
        big[3],
        pieces[2],
        big[2],
        pieces[3],
        pieces[4],
        pieces[5],
        big[1],
        pieces[6],
        big[0],
        pieces[7],
    )


def solution(mesh):
    both = ("dp", "seq")
    token_spec = P(None, both, None)
    vector, matrix = P(both), P(both, None)
    in_specs = (
        token_spec,
        token_spec,
        P(None, "dp", None),
        vector,
        vector,
        matrix,
        vector,
        matrix,
        vector,
        vector,
        vector,
        matrix,
        vector,
        matrix,
        vector,
    )
    out_specs = (
        token_spec,
        token_spec,
        vector,
        vector,
        matrix,
        vector,
        matrix,
        vector,
        vector,
        vector,
        matrix,
        vector,
        matrix,
        vector,
    )
    return jax.shard_map(local, mesh=mesh, in_specs=in_specs, out_specs=out_specs, check_vma=False)
```

profile of v0, /device:TPU:9, one launch (start us, length us, event | category | flops | bytes accessed | tf_op | source)
XLA Modules:
  0.0 637.0 jit_solution(17475978828896782103)
XLA Ops:
  7.2 5.5 concatenate.45
  22.6 18.3 %collective-permute-done = bf16[512,768]{1,0:T(8,128)(2,1)} collective-permute-done((bf16[512,768]{1,0:T(8,128)(2,1)S(1)}, bf16[512,768]{1,0:T(8,128)(2,1)}, u32[]{:S(2)}, u32[]{:S(2)}) %collective-permute-start) | collective-permute-done | bytes 786464 | tf_op jit(solution)/shard_map/ppermute | solution.py:269
  47.6 2.1 select_bitcast_fusion.1
  51.4 31.5 %all-gather.3.cloned.1.call-done = bf16[1024,2304]{1,0:T(8,128)(2,1)} async-done(((bf16[32,2304]{1,0:T(8,128)(2,1)}), bf16[1024,2304]{1,0:T(8,128)(2,1)}) %all-gather.3.cloned.1.call-update) | async-done | bytes 4718608 | tf_op jit(solution)/shard_map/all_gather | solution.py:230
  84.4 4.0 slice.247
  89.6 1.6 constant_dynamic-slice_fusion.5
  92.6 5.8 add_convert_fusion.q_ref.k_ref.v_ref
  98.4 59.9 %attend_forward.1 = (bf16[2048,384]{1,0:T(8,128)(2,1)}, f32[3,2,2048]{2,1,0:T(2,128)}) custom-call(s32[8]{0:T(128)} %copy-done.42, bf16[2048,1152]{1,0:T(8,128)(2,1)} %add_convert_fusion.q_ref.k_ref.v_ref, bf16[2048,1152]{1,0:T(8,128)(2,1)} %add_convert_fusion.q_ref.k_ref.v_ref, bf16[2048,1152]{1,0:T(8,128)(2,1)} %add_convert_fusion.q_ref.k_ref.v_ref, ...), custom_call_target="tpu_custom_call" | custom-call | flops 3221225472 | bytes 7077888 | tf_op jit(solution)/shard_map/attend_forward/pallas_call | solution.py:106
  158.4 2.1 dynamic-slice_bitcast_fusion.4
  163.3 1.7 fusion.67
  165.5 1.7 bitcast_select_fusion.7
  168.5 3.5 all-gather.5.cloned.1.call-done
  172.0 2.6 slice.260
  174.7 4.8 fusion.70
  182.2 9.7 %fusion.39 = f32[1024,3072]{1,0:T(8,128)} fusion(bf16[768,768]{1,0:T(8,128)(2,1)S(1)} %bitcast.270, bf16[768,768]{1,0:T(8,128)(2,1)S(1)} %bitcast.272, bf16[768,768]{1,0:T(8,128)(2,1)S(1)} %bitcast.274, bf16[768,768]{1,0:T(8,128)(2,1)S(1)} %bitcast.268, f32[1024,768]{1,0:T(8,128)S(1)} %get-tuple-element.105, f32[768]{0:T(1024)S(1)} %reshape.765, ...), kind=kOutput, calls=%fused_computation.87 | convolution fusion | flops 4854644736 | bytes 20461568 | tf_op jit(solution)/shard_map/dot_general | solution.py:347
  191.9 16.8 %fusion.77 = (bf16[3072]{0:T(1024)(128)(2,1)S(1)}, bf16[1024,3072]{1,0:T(8,128)(2,1)}) fusion(f32[1024,3072]{1,0:T(8,128)} %fusion.39, f32[3072]{0:T(1024)S(1)} %reshape.766, bf16[1024,768]{1,0:T(8,128)(2,1)S(1)} %bitcast.265, bf16[3072,768]{1,0:T(8,128)(2,1)S(1)} %bitcast.249), kind=kOutput, calls=%fused_computation.217 | convolution fusion | flops 4901041152 | bytes 25184256 | tf_op jit(solution)/shard_map/dot_general | solution.py:26
  208.7 8.4 %multiply_reduce_fusion.1 = (bf16[768]{0:T(1024)(128)(2,1)S(1)}, f32[1024]{0:T(1024)S(1)}, bf16[768]{0:T(1024)(128)(2,1)S(1)}, f32[1024,768]{1,0:T(8,128)S(1)}) fusion(f32[1024,768]{1,0:T(8,128)S(1)} %get-tuple-element.105, f32[1024]{0:T(1024)S(1)} %fusion.48, f32[1024]{0:T(1024)S(1)} %broadcast_multiply_fusion.2, f32[768]{0:T(1024)S(1)} %reshape.764, ...), kind=kOutput, calls=%fused_computation.51 | convolution fusion | flops 4857000960 | bytes 17319936 | tf_op jit(solution)/shard_map/dot_general | solution.py:26
  221.5 2.7 convolution_convert_fusion.2
  224.1 4.4 reshape.737
  228.5 6.3 constant_dynamic-slice_fusion.1
  236.2 2.6 add_convert_fusion.1
  239.2 3.4 convolution_convert_fusion.3
  246.7 57.5 %attend_backward.1 = bf16[3,2048,384]{2,1,0:T(8,128)(2,1)} custom-call(s32[8]{0:T(128)} %convert_reduce_fusion.4.high_ref, bf16[2048,1152]{1,0:T(8,128)(2,1)} %add_convert_fusion.q_ref.k_ref.v_ref, bf16[2048,1152]{1,0:T(8,128)(2,1)} %add_convert_fusion.q_ref.k_ref.v_ref, bf16[2048,1152]{1,0:T(8,128)(2,1)} %add_convert_fusion.q_ref.k_ref.v_ref, ...), custom_call_target="tpu_custom_call" | custom-call | flops 8053063680 | bytes 14155776 | tf_op jit(solution)/shard_map/attend_backward/pallas_call | solution.py:198
  304.2 3.2 convert_reduce_fusion
  307.9 1.8 fusion.33
  309.8 1.8 fusion.31
  311.7 2.3 select_dynamic-update-slice_fusion.5
  313.9 1.9 add_convert_fusion.2
  315.9 1.7 copy-done.18
  320.4 3.7 select_dynamic-update-slice_fusion.3
  324.9 3.7 select_dynamic-update-slice_fusion.1
  329.5 6.1 copy.49
  335.7 3.2 fusion.20
  339.0 1.7 copy-done.6
  340.6 1.6 fusion.23
  342.9 1.7 copy-done.9
  344.6 2.8 pad_maximum_fusion.1
  347.4 9.1 %convolution_convert_fusion.1 = bf16[768,3072]{1,0:T(8,128)(2,1)S(1)} fusion(bf16[1024,3072]{1,0:T(8,128)(2,1)} %get-tuple-element.108, f32[1024,768]{1,0:T(8,128)} %copy-done.10, f32[768]{0:T(1024)S(1)} %reshape.765, f32[768]{0:T(1024)S(1)} %reshape.764, f32[1024]{0:T(1024)S(1)} %fusion.48, f32[1024]{0:T(1024)S(1)} %broadcast_multiply_fusion.2), kind=kOutput, calls=%fused_computation.22 | convolution fusion | flops 4838129664 | bytes 14170112 | tf_op jit(solution)/shard_map/dot_general | solution.py:22
  362.3 3.8 multiply_convert_fusion.1
  366.1 8.1 %convolution_convert_fusion = bf16[3072,768]{1,0:T(8,128)(2,1)S(1)} fusion(bf16[1024,768]{1,0:T(8,128)(2,1)S(1)} %get-tuple-element.65, f32[1024,3072]{1,0:T(8,128)S(1)} %bitcast.295, f32[3072]{0:T(1024)S(1)} %reshape.766), kind=kOutput, calls=%fused_computation.21 | convolution fusion | flops 4865654784 | bytes 18886656 | tf_op jit(solution)/shard_map/dot_general | solution.py:22
  374.2 2.5 constant_dynamic-update-slice_fusion.6
  378.7 12.8 %multiply_convert_fusion.4 = bf16[1024,768]{1,0:T(8,128)(2,1)S(1)} fusion(f32[1024,768]{1,0:T(8,128)S(1)} %copy-done.11, bf16[3072,768]{1,0:T(8,128)(2,1)} %bitcast.250, f32[1024]{0:T(1024)S(1)} %bitcast.282, f32[768]{0:T(1024)S(1)} %reshape.767, f32[1024,3072]{1,0:T(8,128)} %fusion.39, f32[3072]{0:T(1024)S(1)} %reshape.766), kind=kOutput, calls=%fused_computation.56 | convolution fusion | flops 4867227648 | bytes 22039552 | tf_op jit(solution)/shard_map/dot_general | solution.py:350
  391.6 18.0 %collective-permute-start.3 = (bf16[512,768]{1,0:T(8,128)(2,1)S(1)}, bf16[512,768]{1,0:T(8,128)(2,1)S(1)}, u32[]{:S(2)}, u32[]{:S(2)}) collective-permute-start(bf16[512,768]{1,0:T(8,128)(2,1)S(1)} %dynamic-slice_bitcast_fusion.3), channel_id=1, source_target_pairs={{0,2},{1,3},{2,0},{3,1},{4,6},{5,7},{6,4},{7,5},{8,10},{9,11},{10,... | collective-permute-start | bytes 2359304 | tf_op jit(solution)/shard_map/ppermute | solution.py:275
  409.8 26.0 %collective-permute-done.3 = bf16[512,768]{1,0:T(8,128)(2,1)S(1)} collective-permute-done((bf16[512,768]{1,0:T(8,128)(2,1)S(1)}, bf16[512,768]{1,0:T(8,128)(2,1)S(1)}, u32[]{:S(2)}, u32[]{:S(2)}) %collective-permute-start.3) | collective-permute-done | bytes 786464 | tf_op jit(solution)/shard_map/ppermute | solution.py:275
  437.2 19.6 %collective-permute-done.7 = bf16[512,768]{1,0:T(8,128)(2,1)S(1)} collective-permute-done((bf16[512,768]{1,0:T(8,128)(2,1)S(1)}, bf16[512,768]{1,0:T(8,128)(2,1)S(1)}, u32[]{:S(2)}, u32[]{:S(2)}) %collective-permute-start.7) | collective-permute-done | bytes 786464 | tf_op jit(solution)/shard_map/ppermute | solution.py:275
  458.2 21.0 %reduce-scatter.3.cloned.1.call-done = bf16[32,2304]{1,0:T(8,128)(2,1)} async-done(((bf16[1024,2304]{1,0:T(8,128)(2,1)}), bf16[32,2304]{1,0:T(8,128)(2,1)}) %reduce-scatter.3.cloned.1.call-update) | async-done | bytes 147472 | tf_op jit(solution)/shard_map/reduce_scatter | solution.py:234
  483.5 142.6 %reduce-scatter.5.cloned.1.call-done = bf16[216,768]{1,0:T(8,128)(2,1)} async-done(((bf16[6912,768]{1,0:T(8,128)(2,1)}), bf16[216,768]{1,0:T(8,128)(2,1)}) %reduce-scatter.5.cloned.1.call-update) | async-done | bytes 331792 | tf_op jit(solution)/shard_map/reduce_scatter | solution.py:234
  628.4 1.6 slice.284
  (221 shorter events, 62.2 us)
Async XLA Ops:
  7.2 33.8 %copy-start.32 = (bf16[2,512,768]{2,1,0:T(8,128)(2,1)S(1)}, bf16[2,512,768]{2,1,0:T(8,128)(2,1)}, u32[]{:S(2)}) copy-start(bf16[2,512,768]{2,1,0:T(8,128)(2,1)} %param.15) | copy-start | bytes 4718596
  7.2 75.7 %all-gather.3.cloned.1.call-start = ((), (), s32[]{:S(2)}) async-start(), calls=%async_computation.2 | async-start | bytes 4866048 | tf_op jit(solution)/shard_map/all_gather | solution.py:230
  14.5 157.5 %all-gather.5.cloned.1.call-start = ((), (), s32[]{:S(2)}) async-start(), calls=%async_computation.3 | async-start | bytes 10948608 | tf_op jit(solution)/shard_map/all_gather | solution.py:230
  20.1 459.2 %reduce-scatter.3.cloned.1.call-start = ((), (), s32[]{:S(2)}) async-start(), calls=%async_computation.4 | async-start | bytes 4866048 | tf_op jit(solution)/shard_map/reduce_scatter | solution.py:234
  21.3 19.6 %collective-permute-start = (bf16[512,768]{1,0:T(8,128)(2,1)S(1)}, bf16[512,768]{1,0:T(8,128)(2,1)}, u32[]{:S(2)}, u32[]{:S(2)}) collective-permute-start(bf16[512,768]{1,0:T(8,128)(2,1)S(1)} %dynamic-slice_bitcast_fusion.5), channel_id=1, source_target_pairs={{0,2},{1,3},{2,0},{3,1},{4,6},{5,7},{6,4},{7,5},{8,10},{9,11},{10,... | collective-permute-start | bytes 2359304 | tf_op jit(solution)/shard_map/ppermute | solution.py:269
  22.6 21.4 %copy-start.33 = (bf16[2,512,768]{2,1,0:T(8,128)(2,1)S(1)}, bf16[2,512,768]{2,1,0:T(8,128)(2,1)}, u32[]{:S(2)}) copy-start(bf16[2,512,768]{2,1,0:T(8,128)(2,1)} %param.16) | copy-start | bytes 4718596
  42.2 5.4 copy-start
  42.2 5.4 copy-start.2
  42.2 4.0 copy-start.41
  42.4 5.2 copy-start.29
  42.4 5.2 collective-permute-start.1
  44.9 115.9 %collective-permute-start.4 = (bf16[512,768]{1,0:T(8,128)(2,1)}, bf16[512,768]{1,0:T(8,128)(2,1)}, u32[]{:S(2)}, u32[]{:S(2)}) collective-permute-start(bf16[512,768]{1,0:T(8,128)(2,1)} %dynamic-slice_bitcast_fusion.2), channel_id=1, source_target_pairs={{0,2},{1,3},{2,0},{3,1},{4,6},{5,7},{6,4},{7,5},{8,10},{9,11},{10,... | collective-permute-start | bytes 2359304 | tf_op jit(solution)/shard_map/ppermute | solution.py:269
  46.5 3.2 copy-start.40
  46.7 3.0 copy-start.42
  160.5 5.0 collective-permute-start.2
  162.4 2.6 copy-start.15
  174.6 17.3 %copy-start.21 = (bf16[32,96,768]{2,1,0:T(8,128)(2,1)}, bf16[32,96,768]{2,1,0:T(8,128)(2,1)S(1)}, u32[]{:S(2)}) copy-start(bf16[32,96,768]{2,1,0:T(8,128)(2,1)S(1)} %slice.260) | copy-start | bytes 14155780
  174.6 4.9 copy-start.30
  174.7 5.3 copy-start.31
  179.5 2.7 copy-start.36
  181.6 35.6 %copy-start.10 = (f32[1024,768]{1,0:T(8,128)}, f32[1024,768]{1,0:T(8,128)S(1)}, u32[]{:S(2)}) copy-start(f32[1024,768]{1,0:T(8,128)S(1)} %get-tuple-element.105) | copy-start | bytes 9437188
  182.2 9.8 %copy-start.34 = (bf16[2,512,768]{2,1,0:T(8,128)(2,1)S(1)}, bf16[2,512,768]{2,1,0:T(8,128)(2,1)}, u32[]{:S(2)}) copy-start(bf16[2,512,768]{2,1,0:T(8,128)(2,1)} %get-tuple-element.33) | copy-start | bytes 4718596
  191.9 16.8 %copy-start.37 = (bf16[32,24,768]{2,1,0:T(8,128)(2,1)S(1)}, bf16[32,24,768]{2,1,0:T(8,128)(2,1)}, u32[]{:S(2)}) copy-start(bf16[32,24,768]{2,1,0:T(8,128)(2,1)} %copy-done.36) | copy-start | bytes 3538948
  236.0 7.8 %collective-permute-start.5 = (bf16[2,512,384]{2,1,0:T(8,128)(2,1)}, bf16[2,512,384]{2,1,0:T(8,128)(2,1)}, u32[]{:S(2)}, u32[]{:S(2)}) collective-permute-start(bf16[2,512,384]{2,1,0:T(8,128)(2,1)} %bitcast.232), channel_id=1, source_target_pairs={{0,1},{1,0},{2,3},{3,2},{4,5},{5,4},{6,7},{7,6},{8,9},{9,8},{10,11... | collective-permute-start | bytes 2359304 | tf_op jit(solution)/shard_map/ppermute | solution.py:379
  239.2 4.6 copy-start.20
  246.7 60.7 %copy-start.28 = (bf16[768,384]{1,0:T(8,128)(2,1)S(1)}, bf16[768,384]{1,0:T(8,128)(2,1)}, u32[]{:S(2)}) copy-start(bf16[768,384]{1,0:T(8,128)(2,1)} %copy-done.27) | copy-start | bytes 1769476
  304.2 3.8 copy-start.8
  307.9 1.8 copy-start.26
  309.8 1.9 copy-start.22
  311.7 2.3 copy-start.24
  315.9 1.7 copy-start.18
  318.8 16.9 %collective-permute-start.6 = (bf16[2,512,768]{2,1,0:T(8,128)(2,1)}, bf16[2,512,768]{2,1,0:T(8,128)(2,1)}, u32[]{:S(2)}, u32[]{:S(2)}) collective-permute-start(bf16[2,512,768]{2,1,0:T(8,128)(2,1)} %dynamic-slice_bitcast_fusion), channel_id=1, source_target_pairs={{0,1},{1,0},{2,3},{3,2},{4,5},{5,4},{6,7},{7,6},{8,9},{9,8},{10,11... | collective-permute-start | bytes 4718600 | tf_op jit(solution)/shard_map/ppermute | solution.py:391
  329.5 6.2 copy-start.1
  329.5 6.2 copy-start.3
  338.9 1.7 copy-start.6
  342.6 2.0 copy-start.9
  347.4 278.8 %reduce-scatter.5.cloned.1.call-start = ((), (), s32[]{:S(2)}) async-start(), calls=%async_computation.5 | async-start | bytes 10948608 | tf_op jit(solution)/shard_map/reduce_scatter | solution.py:234
  347.4 18.7 %slice-start = ((s8[12582912]{0:T(1024)(128)(4,1)}), s8[4194304]{0:T(1024)(128)(4,1)S(1)}, s32[]{:S(2)}) async-start(s8[12582912]{0:T(1024)(128)(4,1)} %bitcast.294), calls=%async_computation.6 | async-start | bytes 8388608
  347.4 18.7 %slice-start.1 = ((s8[12582912]{0:T(1024)(128)(4,1)}), s8[4194304]{0:T(1024)(128)(4,1)S(1)}, s32[]{:S(2)}) async-start(s8[12582912]{0:T(1024)(128)(4,1)} %bitcast.294), calls=%async_computation.7 | async-start | bytes 8388608
  356.9 4.5 copy-start.17
  358.0 3.4 copy-start.5
  358.0 4.2 copy-start.7
  358.0 4.3 copy-start.14
  359.1 6.9 %slice-start.2 = ((s8[12582912]{0:T(1024)(128)(4,1)}), s8[4194304]{0:T(1024)(128)(4,1)S(1)}, s32[]{:S(2)}) async-start(s8[12582912]{0:T(1024)(128)(4,1)} %bitcast.294), calls=%async_computation.8 | async-start | bytes 8388608
  376.7 2.0 copy-start.11
  378.7 30.9 %copy-start.19 = (bf16[1024,768]{1,0:T(8,128)(2,1)S(1)}, bf16[1024,768]{1,0:T(8,128)(2,1)}, u32[]{:S(2)}) copy-start(bf16[1024,768]{1,0:T(8,128)(2,1)} %get-tuple-element.66) | copy-start | bytes 4718596
  391.6 44.2 %collective-permute-start.3 = (bf16[512,768]{1,0:T(8,128)(2,1)S(1)}, bf16[512,768]{1,0:T(8,128)(2,1)S(1)}, u32[]{:S(2)}, u32[]{:S(2)}) collective-permute-start(bf16[512,768]{1,0:T(8,128)(2,1)S(1)} %dynamic-slice_bitcast_fusion.3), channel_id=1, source_target_pairs={{0,2},{1,3},{2,0},{3,1},{4,6},{5,7},{6,4},{7,5},{8,10},{9,11},{10,... | collective-permute-start | bytes 2359304 | tf_op jit(solution)/shard_map/ppermute | solution.py:275
  409.7 47.1 %collective-permute-start.7 = (bf16[512,768]{1,0:T(8,128)(2,1)S(1)}, bf16[512,768]{1,0:T(8,128)(2,1)S(1)}, u32[]{:S(2)}, u32[]{:S(2)}) collective-permute-start(bf16[512,768]{1,0:T(8,128)(2,1)S(1)} %dynamic-slice_bitcast_fusion.1), channel_id=1, source_target_pairs={{0,2},{1,3},{2,0},{3,1},{4,6},{5,7},{6,4},{7,5},{8,10},{9,11},{10,... | collective-permute-start | bytes 2359304 | tf_op jit(solution)/shard_map/ppermute | solution.py:275
  (10 other events, 12.3 us)
Sparse Core Ops, SparseCore 0:
  14.6 68.2 all-gather.2
  85.8 86.1 all-gather.4
  347.5 131.6 reduce-scatter.2
  485.1 140.9 reduce-scatter.4
where the time goes:
time: 646 us; the launch traced here: 637 us
  waiting for transfers between devices  263 us (41%)
  Pallas kernels  117 us (18%)
  matrix products  93.7 us (15%)
  local copies, waits for them, and re-layouts  79.8 us (12%)
  other arithmetic  45 us (7%)
  starting transfers between devices  23.3 us (4%)
  between operations  15.1 us (2%)
    reduce_scatter x2, waiting for transfers between devices, scatter_sum(): lax.psum_scatter(full, ('dp', 'seq'), scatter_dimension=0, tiled=True)  164 us
    pallas_call x1, Pallas kernels, attend_forward(): pl.pallas_call(attend_kernel, name='attend_forward', out_shape=(jax.Shape...  59.9 us
    pallas_call x1, Pallas kernels, attend_backward(): pl.pallas_call(attend_back_kernel, name='attend_backward', out_shape=jax....  57.5 us
    ppermute x2, waiting for transfers between devices, home_micro(): came = lax.ppermute(sent, 'seq', swap_micro)  45.6 us
    all_gather x2, waiting for transfers between devices, gather_rows(): return lax.all_gather(shard, ('dp', 'seq'), axis=0, tiled=True)  34.9 us
    dot_general x6, matrix products, against_rows(): lax.dot_general(first, second, (((1,), (1,)), ((), ())), preferred_elemen...  33.5 us
    dot_general x6, matrix products, outer_sum(): lax.dot_general(first, second, (((0,), (0,)), ((), ())), preferred_elemen...  30.3 us
    unnamed x112, local copies, waits for them, and re-layouts  23.5 us
  transfers between devices with their start and end apart: 12, of which 7 were waited for; matrix products, arithmetic and copies ran while one was open for 17% of the time, Pallas kernels for 9%

commit v1 on v0

--- a/solution.py
+++ b/solution.py
@@ -102,7 +102,8 @@
 def attend_forward(packed, low_blocks, begins):
     bucket, columns = packed.shape
     groups = columns // 3 // PAIR
-    tall = lambda first: pl.BlockSpec((bucket, PAIR), lambda g, low: (0, first + g))
+    tall = lambda part: pl.BlockSpec((bucket, PAIR), lambda g, low: (0, 3 * g + part))
+    narrow = pl.BlockSpec((bucket, PAIR), lambda g, low: (0, g))
     return pl.pallas_call(
         attend_kernel,
         name="attend_forward",
@@ -115,11 +116,11 @@
             grid=(groups,),
             in_specs=[
                 tall(0),
-                tall(groups),
-                tall(2 * groups),
+                tall(1),
+                tall(2),
                 pl.BlockSpec((1, bucket), lambda g, low: (0, 0)),
             ],
-            out_specs=[tall(0), pl.BlockSpec((1, 2, bucket), lambda g, low: (g, 0, 0))],
+            out_specs=[narrow, pl.BlockSpec((1, 2, bucket), lambda g, low: (g, 0, 0))],
             scratch_shapes=[pltpu.VMEM((PAIR, bucket), BF16)],
         ),
         cost_estimate=pl.CostEstimate(
@@ -181,37 +182,38 @@
         zero = jnp.zeros((TILE, PAIR), F32)
         state = visit(j, (zero, zero), True)
         state = lax.fori_loop(j + 1, high_ref[j], lambda i, s: visit(i, s, False), state)
-        out_ref[1, there, :] = state[0].astype(BF16)
-        out_ref[2, there, :] = state[1].astype(BF16)
+        out_ref[there, PAIR : 2 * PAIR] = state[0].astype(BF16)
+        out_ref[there, 2 * PAIR :] = state[1].astype(BF16)
         return carry
 
     lax.fori_loop(0, blocks, one_key_block, 0)
     for block in range(blocks):
         at = slice(block * TILE, (block + 1) * TILE)
-        out_ref[0, at, :] = (query_t[:, at].T * HD ** (-0.5)).astype(BF16)
+        out_ref[at, :PAIR] = (query_t[:, at].T * HD ** (-0.5)).astype(BF16)
 
 
 def attend_backward(packed, attended, grad_attended, logsum, high_blocks, begins):
     bucket, columns = packed.shape
     groups = columns // 3 // PAIR
-    tall = lambda first: pl.BlockSpec((bucket, PAIR), lambda g, high: (0, first + g))
+    tall = lambda part: pl.BlockSpec((bucket, PAIR), lambda g, high: (0, 3 * g + part))
+    narrow = pl.BlockSpec((bucket, PAIR), lambda g, high: (0, g))
     return pl.pallas_call(
         attend_back_kernel,
         name="attend_backward",
-        out_shape=jax.ShapeDtypeStruct((3, bucket, columns // 3), BF16),
+        out_shape=jax.ShapeDtypeStruct((bucket, columns), BF16),
         grid_spec=pltpu.PrefetchScalarGridSpec(
             num_scalar_prefetch=1,
             grid=(groups,),
             in_specs=[
                 tall(0),
-                tall(groups),
-                tall(2 * groups),
-                tall(0),
-                tall(0),
+                tall(1),
+                tall(2),
+                narrow,
+                narrow,
                 pl.BlockSpec((1, bucket), lambda g, high: (0, 0)),
                 pl.BlockSpec((1, 2, bucket), lambda g, high: (g, 0, 0)),
             ],
-            out_specs=pl.BlockSpec((3, bucket, PAIR), lambda g, high: (0, 0, g)),
+            out_specs=pl.BlockSpec((bucket, 3 * PAIR), lambda g, high: (0, g)),
             scratch_shapes=[
                 pltpu.VMEM((PAIR, bucket), BF16),
                 pltpu.VMEM((PAIR, bucket), F32),
@@ -224,6 +226,205 @@
             transcendentals=2 * groups * bucket * bucket // 2,
         ),
     )(high_blocks, packed, packed, packed, attended, grad_attended, begins, logsum)
+
+
+def position():
+    dp, seq = lax.axis_index("dp"), lax.axis_index("seq")
+    return lax.div(dp, 2), lax.rem(dp, 2), lax.div(seq, 2), lax.rem(seq, 2)
+
+
+def device(z, x, y, core):
+    return (2 * z + x, 2 * y + core)
+
+
+def send(source, target, semaphores, index, to):
+    leave, arrive = semaphores
+    copy = pltpu.make_async_remote_copy(
+        src_ref=source,
+        dst_ref=target,
+        send_sem=leave.at[index],
+        recv_sem=arrive.at[index],
+        device_id=to,
+        device_id_type=pl.DeviceIdType.MESH,
+    )
+    copy.start()
+    return copy
+
+
+def meet(z, x, y, core):
+    barrier = pltpu.get_barrier_semaphore()
+    others = [device(z, 1 - x, y, core), device(z, x, 1 - y, core), device(z, x, y, 1 - core)]
+    others += [device(lax.rem(z + t, 4), x, y, core) for t in (1, 2, 3)]
+    for other in others:
+        pl.semaphore_signal(barrier, inc=1, device_id=other, device_id_type=pl.DeviceIdType.MESH)
+    pl.semaphore_wait(barrier, len(others))
+
+
+def gather_kernel(token_ref, half_ref, tiny_ref, all_tokens, all_half, all_tiny, local_sem, *semaphores):
+    z, x, y, core = position()
+    token_sems, half_sems, tiny_sems = [semaphores[2 * i : 2 * i + 2] for i in range(3)]
+    meet(z, x, y, core)
+    core_twin, y_twin, x_twin = device(z, x, y, 1 - core), device(z, x, 1 - y, core), device(z, 1 - x, y, core)
+    streams = [
+        (half_ref.at[core], half_ref.at[1 - core], all_half, half_sems),
+        (tiny_ref, tiny_ref, all_tiny, tiny_sems),
+    ]
+    sent = []
+    local = [pltpu.make_async_copy(token_ref.at[y], all_tokens.at[y, core], local_sem.at[2])]
+    for i, (mine, _, whole, _) in enumerate(streams):
+        local.append(pltpu.make_async_copy(mine, whole.at[z, x, y, core], local_sem.at[i]))
+    for copy in local:
+        copy.start()
+    swaps = [send(twins, whole.at[z, x, y, core], sems, 0, core_twin) for _, twins, whole, sems in streams]
+    for copy in local[1:]:
+        copy.wait()
+    for copy in swaps:
+        copy.wait_recv()
+    sent += swaps
+    own = [(whole.at[z, x, y], sems) for _, _, whole, sems in streams]
+    over_y = [send(piece, piece, sems, 1, y_twin) for piece, sems in own]
+    token_y = send(token_ref.at[1 - y], all_tokens.at[y, core], token_sems, 0, y_twin)
+    token_own = send(token_ref.at[y], all_tokens.at[y, core], token_sems, 1, core_twin)
+    along_z, over_x = {}, []
+
+    def spread_piece(p, pieces):
+        for t in (1, 2, 3):
+            for i, (piece, sems) in enumerate(pieces):
+                along_z[p, t, i] = send(piece, piece, sems, 1 + 3 * p + t, device(lax.rem(z + t, 4), x, y, core))
+        for piece, sems in pieces:
+            over_x.append(send(piece, piece, sems, 8 + 4 * p, x_twin))
+
+    spread_piece(0, own)
+    for copy in over_y:
+        copy.wait_recv()
+    spread_piece(1, [(whole.at[z, x, 1 - y], sems) for _, _, whole, sems in streams])
+    token_y.wait_recv()
+    token_next = send(all_tokens.at[1 - y, core], all_tokens.at[1 - y, core], token_sems, 2, core_twin)
+    for p in (0, 1):
+        row = y if p == 0 else 1 - y
+        for t in (1, 2, 3):
+            source = lax.rem(z + 4 - t, 4)
+            for i, (_, _, whole, sems) in enumerate(streams):
+                along_z[p, t, i].wait_recv()
+                piece = whole.at[source, x, row]
+                over_x.append(send(piece, piece, sems, 8 + 4 * p + t, x_twin))
+    for copy in over_x + [token_own, token_next]:
+        copy.wait_recv()
+    for copy in sent + over_y + [token_y, token_own, token_next] + list(along_z.values()) + over_x:
+        copy.wait_send()
+    local[0].wait()
+
+
+def gather_first(tokens, half_shard, tiny_shard):
+    _, local_rows, width = tokens.shape
+    _, rows, half_columns = half_shard.shape
+    anywhere = pl.BlockSpec(memory_space=pl.ANY)
+    near = pl.BlockSpec(memory_space=pltpu.VMEM)
+    sems = pltpu.SemaphoreType.DMA
+    return pl.pallas_call(
+        gather_kernel,
+        name="gather_first",
+        out_shape=(
+            jax.ShapeDtypeStruct((2, 2, local_rows, width), BF16),
+            jax.ShapeDtypeStruct((4, 2, 2, 2, rows, half_columns), BF16),
+            jax.ShapeDtypeStruct((4, 2, 2, 2, 8, 128), F32),
+        ),
+        in_specs=[near, near, near],
+        out_specs=[anywhere, anywhere, anywhere],
+        scratch_shapes=[sems((3,)), sems((3,)), sems((3,)), sems((16,)), sems((16,)), sems((16,)), sems((16,))],
+        compiler_params=pltpu.CompilerParams(collective_id=1, has_side_effects=True),
+    )(tokens, half_shard, tiny_shard)
+
+
+def reduce_kernel(big_ref, tiny_ref, own_ref, other_ref, sum_ref, *scratch):
+    z, x, y, core = position()
+    meet(z, x, y, core)
+    streams = []
+    for i, source in enumerate((big_ref, tiny_ref)):
+        streams.append((source,) + scratch[10 * i : 10 * i + 10])
+    first_twin = device(z, x + (1 - core) * (1 - 2 * x), y + core * (1 - 2 * y), core)
+    second_twin = device(z, x + core * (1 - 2 * x), y + (1 - core) * (1 - 2 * y), core)
+    keep = (1 - core) * y + core * x
+    order = (1, 2, 3, 0)
+    one, two, three = {}, {}, {}
+    for t in order:
+        k = lax.rem(z + t, 4)
+        for j in (0, 1):
+            ix = (1 - core) * (1 - x) + core * j
+            iy = (1 - core) * j + core * (1 - y)
+            for i, (source, came_one, *_, leave, arrive) in enumerate(streams):
+                one[t, j, i] = send(source.at[k, ix, iy], came_one.at[t, j], (leave, arrive), 2 * t + j, first_twin)
+    for t in order:
+        k = lax.rem(z + t, 4)
+        for i, (source, came_one, sum_one, came_two, *_, leave, arrive) in enumerate(streams):
+            for j in (0, 1):
+                one[t, j, i].wait_recv()
+                ix = (1 - core) * x + core * j
+                iy = (1 - core) * j + core * y
+                total = source[k, ix, iy].astype(F32) + came_one[t, j].astype(F32)
+                sum_one[t, j] = total.astype(sum_one.dtype)
+            two[t, i] = send(sum_one.at[t, 1 - keep], came_two.at[t], (leave, arrive), 8 + t, second_twin)
+    for t in order:
+        for i, (_, _, sum_one, came_two, sum_two, came_three, total_ref, _, leave, arrive) in enumerate(
+            [(s[0], s[1], s[2], s[3], s[4], s[5], s[6], s[7], s[9], s[10]) for s in streams]
+        ):
+            two[t, i].wait_recv()
+            total = sum_one[t, keep].astype(F32) + came_two[t].astype(F32)
+            if t == 0:
+                total_ref[...] = total
+            else:
+                sum_two[t - 1] = total.astype(sum_two.dtype)
+                to = device(lax.rem(z + t, 4), x, y, core)
+                three[t, i] = send(sum_two.at[t - 1], came_three.at[t - 1], (leave, arrive), 11 + t, to)
+    last = []
+    for i, s in enumerate(streams):
+        came_three, total_ref, came_last, leave, arrive = s[5], s[6], s[7], s[9], s[10]
+        for t in (1, 2, 3):
+            three[t, i].wait_recv()
+        total_ref[...] += sum(came_three[t].astype(F32) for t in range(3))
+        rows = came_last.shape[0]
+        piece = total_ref if i == 1 else total_ref.at[pl.ds(pl.multiple_of((1 - core) * rows, 8), rows)]
+        last.append(send(piece, came_last, (leave, arrive), 15, device(z, x, y, 1 - core)))
+    rows = own_ref.shape[0]
+    own_ref[...] = streams[0][6][pl.ds(pl.multiple_of(core * rows, 8), rows)]
+    for copy in last:
+        copy.wait_recv()
+    other_ref[...] = streams[0][7][...]
+    sum_ref[...] = streams[1][6][...] + streams[1][7][...]
+    for copy in list(one.values()) + list(two.values()) + list(three.values()) + last:
+        copy.wait_send()
+
+
+def reduce_last(big, tiny):
+    rows, half_columns = big.shape[3:]
+    near = pl.BlockSpec(memory_space=pltpu.VMEM)
+    scratch = []
+    for shape, kind, kept in (((rows, half_columns), BF16, (rows // 2, half_columns)), ((8, 128), F32, (8, 128))):
+        scratch += [
+            pltpu.VMEM((4, 2) + shape, kind),
+            pltpu.VMEM((4, 2) + shape, kind),
+            pltpu.VMEM((4,) + shape, kind),
+            pltpu.VMEM((3,) + shape, kind),
+            pltpu.VMEM((3,) + shape, kind),
+            pltpu.VMEM(shape, F32),
+            pltpu.VMEM(kept, F32),
+            pltpu.SemaphoreType.DMA((1,)),
+            pltpu.SemaphoreType.DMA((16,)),
+            pltpu.SemaphoreType.DMA((16,)),
+        ]
+    return pl.pallas_call(
+        reduce_kernel,
+        name="reduce_last",
+        out_shape=(
+            jax.ShapeDtypeStruct((rows // 2, half_columns), F32),
+            jax.ShapeDtypeStruct((rows // 2, half_columns), F32),
+            jax.ShapeDtypeStruct((8, 128), F32),
+        ),
+        in_specs=[near, near],
+        out_specs=[near, near, near],
+        scratch_shapes=scratch,
+        compiler_params=pltpu.CompilerParams(collective_id=2, has_side_effects=True),
+    )(big, tiny)
 
 
 def gather_rows(shard):
@@ -279,21 +480,43 @@
         first, second = jnp.where(core == 0, own, other), jnp.where(core == 0, other, own)
         return jnp.stack([first, second], axis=1).reshape((bucket,) + own.shape[2:])
 
-    own_tokens = own_micro(tokens)
     own_cotangent = own_micro(cotangent)
-    other_tokens = lax.ppermute(own_tokens, "seq", swap_core)
 
     vectors = (gain_first, shift_first, packed_bias, output_bias, gain_second, shift_second, expand_bias, reduce_bias)
     sizes = [v.shape[0] for v in vectors]
     small_count = sum(sizes)
     pieces_per_row = hidden_width // width
     rows = output_weight.shape[0]
-    extra = jnp.pad(jnp.concatenate(vectors), (0, 8 * 3 * width - small_count)).reshape(8, 3 * width)
-    first = gather_rows(jnp.concatenate([packed_weight, extra])).reshape(devices, rows + 8, 3 * width)
+    blocks = columns // PAIR
+    tiny = jnp.pad(jnp.concatenate(vectors).astype(F32), (0, 1024 - small_count)).reshape(8, 128)
+    halves = jnp.stack(
+        [
+            jnp.concatenate(
+                [
+                    packed_weight[:, part * width + c * columns + g * PAIR :][:, :PAIR]
+                    for g in range(blocks)
+                    for part in range(3)
+                ],
+                axis=1,
+            )
+            for c in range(share)
+        ]
+    )
+    own_kernels = devices == 32 and groups == 4
+    if own_kernels:
+        all_tokens, half_packed, all_tiny = gather_first(tokens, halves, tiny)
+        everyone = all_tokens.reshape(bucket, width)
+        own_tokens = lax.dynamic_index_in_dim(all_tokens, core, 1, keepdims=False)
+        half_packed = half_packed.reshape(width, 3 * columns)
+    else:
+        own_tokens = own_micro(tokens)
+        everyone = interleave(own_tokens, lax.ppermute(own_tokens, "seq", swap_core))
+        half_packed = lax.all_gather(halves, ("dp", "seq"), axis=1, tiled=True)
+        half_packed = lax.dynamic_index_in_dim(half_packed, core, 0, keepdims=False)
+        all_tiny = gather_rows(tiny)
+    small_all = all_tiny.reshape(devices, 1024)
     expand_blocks = [expand_weight[:, j * width : (j + 1) * width] for j in range(pieces_per_row)]
     second = gather_rows(jnp.concatenate([output_weight] + expand_blocks + [reduce_weight])).reshape(devices, -1, width)
-    full_packed = first[:, :rows].reshape(width, 3 * width)
-    small_all = first[:, rows]
     full_output = second[:, :rows].reshape(width, width)
     full_expand = jnp.concatenate(
         [second[:, rows * (j + 1) : rows * (j + 2)].reshape(width, width) for j in range(pieces_per_row)], axis=1
@@ -301,7 +524,7 @@
     full_reduce = second[:, rows * (pieces_per_row + 1) :].reshape(hidden_width, width)
     pieces, at = [], 0
     for size in sizes:
-        pieces.append(small_all[:, at : at + size].reshape(-1).astype(F32))
+        pieces.append(small_all[:, at : at + size].reshape(-1))
         at += size
     gain_one, shift_one, packed_shift, output_shift, gain_two, shift_two, expand_shift, reduce_shift = pieces
 
@@ -319,15 +542,10 @@
     valid = lax.dynamic_index_in_dim(valid_all, core, 1, keepdims=False).reshape(-1, 1)
 
     inputs = own_tokens.reshape(-1, width).astype(F32)
-    everyone = interleave(own_tokens, other_tokens).astype(F32)
-    normed_low = layer_norm(everyone, gain_one, shift_one).astype(BF16)
-    half_packed = jnp.concatenate(
-        [lax.dynamic_slice(full_packed, (0, part * width + core * columns), (width, columns)) for part in range(3)], axis=1
-    )
+    normed_low = layer_norm(everyone.astype(F32), gain_one, shift_one).astype(BF16)
     bias_row = jnp.concatenate([packed_shift[:width], jnp.zeros((width,), F32), packed_shift[width:]])
-    half_bias = jnp.concatenate(
-        [lax.dynamic_slice(bias_row, (part * width + core * columns,), (columns,)) for part in range(3)]
-    )
+    bias_row = bias_row.reshape(3, share, blocks, PAIR)
+    half_bias = jnp.swapaxes(lax.dynamic_index_in_dim(bias_row, core, 1, keepdims=False), 0, 1).reshape(-1)
     packed = (jnp.dot(normed_low, half_packed, preferred_element_type=F32) + half_bias).astype(BF16)
     attended_heads, logsum = attend_forward(packed, low_blocks, begins)
 
@@ -373,19 +591,17 @@
         + [reduce_weight_grad.astype(BF16).reshape(devices, -1, width)],
         axis=1,
     )
-    early_sum = scatter_sum(early.reshape(-1, width)).astype(F32)
     grad_attended = against_rows(grad_proj, full_output).astype(BF16).reshape(2, local_rows, share, columns)
     kept = lax.dynamic_index_in_dim(grad_attended, core, 2, keepdims=False)
     came = lax.ppermute(
         lax.dynamic_index_in_dim(grad_attended, 1 - core, 2, keepdims=False), "seq", swap_core
     )
-    grad_heads = interleave(kept, came)
+    grad_heads, early = lax.optimization_barrier((interleave(kept, came), early))
+    early_sum = scatter_sum(early.reshape(-1, width)).astype(F32)
     grad_packed = attend_backward(packed, attended_heads, grad_heads, logsum, high_blocks, begins)
-    half_grads = [outer_sum(normed_low, grad_packed[part]).astype(BF16) for part in range(3)]
-    half_sums = jnp.sum(grad_packed.astype(F32), axis=1)
-    part_grad = sum(
-        against_rows(grad_packed[part], half_packed[:, part * columns : (part + 1) * columns]) for part in range(3)
-    ).astype(BF16)
+    half_grad = outer_sum(normed_low, grad_packed).astype(BF16)
+    half_sums = jnp.sum(grad_packed.astype(F32), axis=0).reshape(blocks, 3, PAIR)
+    part_grad = against_rows(grad_packed, half_packed).astype(BF16)
     by_core = part_grad.reshape(2, share, local_rows, width)
     kept = lax.dynamic_index_in_dim(by_core, core, 1, keepdims=False)
     came = lax.ppermute(lax.dynamic_index_in_dim(by_core, 1 - core, 1, keepdims=False), "seq", swap_core)
@@ -401,16 +617,32 @@
         nothing = jnp.zeros_like(half)
         return [jnp.where(core == place_of, half, nothing) for place_of in range(share)]
 
-    half_places = [block for half in half_grads for block in spread(half)]
-    packed_bias_grad = jnp.concatenate([block for part in (0, 2) for block in spread(half_sums[part])])
+    packed_bias_grad = jnp.concatenate([block for part in (0, 2) for block in spread(half_sums[:, part].reshape(-1))])
     small_grads = [gain_one_grad, shift_one_grad, packed_bias_grad, output_bias_grad, gain_two_grad, shift_two_grad, expand_bias_grad, reduce_bias_grad]
-    small_rows = jnp.concatenate([g.reshape(devices, -1) for g in small_grads], axis=1).astype(BF16)
-    small_rows = jnp.pad(small_rows, ((0, 0), (0, 8 * 3 * width - small_count))).reshape(devices, 8, 3 * width)
-    last = jnp.concatenate(
-        [jnp.concatenate(half_places, axis=1).reshape(devices, rows, 3 * width), small_rows], axis=1
-    )
-    last_sum = scatter_sum(last.reshape(-1, 3 * width)).astype(F32)
-    small_sum = last_sum[rows]
+    if own_kernels:
+        chips = devices // share
+        small_rows = jnp.concatenate([g.reshape(chips, -1) for g in small_grads], axis=1)
+        small_rows = jnp.pad(small_rows, ((0, 0), (0, 1024 - share * small_count))).reshape(4, 2, 2, 8, 128)
+        own_half, other_half, small_sum = reduce_last(half_grad.reshape(4, 2, 2, share * rows, 3 * columns), small_rows)
+        packed_halves = [jnp.where(core == c, own_half, other_half) for c in range(share)]
+        chip_sum, at, small_sum = small_sum.reshape(-1), 0, []
+        for size in sizes:
+            small_sum.append(lax.dynamic_slice(chip_sum, (at + core * size,), (size,)))
+            at += share * size
+        small_sum = jnp.concatenate(small_sum)
+    else:
+        both_halves = scatter_sum(jnp.concatenate(spread(half_grad), axis=1)).astype(F32)
+        packed_halves = [both_halves[:, c * 3 * columns : (c + 1) * 3 * columns] for c in range(share)]
+        small_sum = scatter_sum(jnp.concatenate([g.reshape(devices, -1) for g in small_grads], axis=1))[0]
+    packed_sum = jnp.concatenate(
+        [
+            packed_halves[c][:, (3 * g + part) * PAIR : (3 * g + part + 1) * PAIR]
+            for part in range(3)
+            for c in range(share)
+            for g in range(blocks)
+        ],
+        axis=1,
+    )
     pieces, at = [], 0
     for size in sizes:
         pieces.append(small_sum[at : at + size])
@@ -418,7 +650,7 @@
     expand_sum = jnp.concatenate(
         [early_sum[rows * (j + 1) : rows * (j + 2)] for j in range(pieces_per_row)], axis=1
     )
-    big = (early_sum[rows * (pieces_per_row + 1) :], expand_sum, early_sum[:rows], last_sum[:rows])
+    big = (early_sum[rows * (pieces_per_row + 1) :], expand_sum, early_sum[:rows], packed_sum)
     return (
         layer_output,
         input_grad,

time: 646 us -> 477 us (0.74)
  waiting for transfers between devices: 263 us -> 14.7 us
  Pallas kernels: 117 us -> 229 us
  starting transfers between devices: 23.3 us -> 2.7 us
  other arithmetic: 45 us -> 37.2 us
    reduce_scatter x2 -> x1, waiting for transfers between devices: 164 us -> 0.01 us  [scatter_sum(): lax.psum_scatter(full, ('dp', 'seq'), scatter_dimension=0, tiled=True)]
    pallas_call x0 -> x2, Pallas kernels: none -> 90.9 us  [the longest x1 50.2 us: gather_first(): pl.pallas_call(gather_kernel, name='gather_first', out_shape=(jax.ShapeDt...]
    ppermute x2, waiting for transfers between devices: 45.6 us -> 0.01 us  [home_micro(): came = lax.ppermute(sent, 'seq', swap_micro)]
    all_gather x2 -> x1, waiting for transfers between devices: 34.9 us -> 0.01 us  [gather_rows(): return lax.all_gather(shard, ('dp', 'seq'), axis=0, tiled=True)]
    ppermute x2, starting transfers between devices: 18.1 us -> 0.07 us  [home_micro(): came = lax.ppermute(sent, 'seq', swap_micro)]
    pallas_call x1, Pallas kernels: 59.9 us -> 70.4 us  [attend_forward(): pl.pallas_call(attend_kernel, name='attend_forward', out_shape=(jax.Shape...]
    pallas_call x1, Pallas kernels: 57.5 us -> 67.5 us  [attend_backward(): pl.pallas_call(attend_back_kernel, name='attend_backward', out_shape=jax....]
    slice x8 -> x2, local copies, waits for them, and re-layouts: 8.87 us -> 0.15 us  [local(): pieces.append(small_all[:, at:at + size].reshape(-1))]
  transfers between devices with their start and end apart: 12 -> 8, of which waited for: 7 -> 1; matrix products, arithmetic and copies ran while one was open for 17% -> 23% of each run, Pallas kernels for 9% -> 49%
where the time goes in v1:
time: 477 us; the launch traced here: 469 us
  Pallas kernels  229 us (48%)
  matrix products  96 us (20%)
  local copies, waits for them, and re-layouts  74.8 us (16%)
  other arithmetic  37.2 us (8%)
  between operations  15.2 us (3%)
  waiting for transfers between devices  14.7 us (3%)
    pallas_call x1, Pallas kernels, attend_forward(): pl.pallas_call(attend_kernel, name='attend_forward', out_shape=(jax.Shape...  70.4 us
    pallas_call x1, Pallas kernels, attend_backward(): pl.pallas_call(attend_back_kernel, name='attend_backward', out_shape=jax....  67.5 us
    pallas_call x1, Pallas kernels, gather_first(): pl.pallas_call(gather_kernel, name='gather_first', out_shape=(jax.ShapeDt...  50.2 us
    pallas_call x1, Pallas kernels, reduce_last(): pl.pallas_call(reduce_kernel, name='reduce_last', out_shape=(jax.ShapeDty...  40.7 us
    dot_general x4, matrix products, against_rows(): lax.dot_general(first, second, (((1,), (1,)), ((), ())), preferred_elemen...  36.8 us
    dot_general x4, matrix products, outer_sum(): lax.dot_general(first, second, (((0,), (0,)), ((), ())), preferred_elemen...  28.6 us
    unnamed x117, local copies, waits for them, and re-layouts  24.7 us
    ppermute x1, waiting for transfers between devices, own_micro(): came = lax.ppermute(sent, 'seq', swap_micro)  14.7 us
  transfers between devices with their start and end apart: 8, of which 1 were waited for; matrix products, arithmetic and copies ran while one was open for 23% of the time, Pallas kernels for 49%

profile of v1, /device:TPU:9, one launch (start us, length us, event | category | flops | bytes accessed | tf_op | source)
XLA Modules:
  0.0 469.4 jit_solution(7658568243427713316)
XLA Ops:
  13.9 5.4 %concatenate.44 = bf16[288]{0:T(512)(128)(2,1)S(1)} concatenate(bf16[24]{0:T(256)(128)(2,1)} %param.18, bf16[24]{0:T(256)(128)(2,1)} %param.19, bf16[48]{0:T(256)(128)(2,1)} %param.21, bf16[24]{0:T(256)(128)(2,1)} %param.23, bf16[24]{0:T(256)(128)(2,1)} %param.24, bf16[24]{0:T(256)(128)(2,1)} %param.25, bf16[96]{0:T(256)(128)(2,1)} %param.27, bf16[24]{0:T(256)(128)(2,1)} %param.29), dimensions={0} | concatenate | bytes 1152 | tf_op jit(solution)/shard_map/concatenate | solution.py:491
  28.4 50.2 %gather_first.1 = (bf16[2,2,512,768]{3,2,1,0:T(8,128)(2,1)}, bf16[4,2,2,2,24,1152]{5,4,3,2,1,0:T(8,128)(2,1)}, f32[4,2,2,2,8,128]{5,4,3,2,1,0:T(8,128)}) custom-call(bf16[2,512,768]{2,1,0:T(8,128)(2,1)} %token_ref.1, bf16[2,24,1152]{2,1,0:T(8,128)(2,1)} %pad_maximum_fusion.9.half_ref, f32[8,128]{1,0:T(8,128)} %bitcast_convert_fusion.tiny_ref), custom_call_target="tpu_custom_call" | custom-call | tf_op jit(solution)/shard_map/gather_first/pallas_call | solution.py:324
  80.9 2.4 convert_reduce_fusion.2
  84.5 1.5 add_convert_fusion.1
  86.0 5.9 %add_convert_fusion.q_ref.k_ref.v_ref = bf16[2048,1152]{1,0:T(8,128)(2,1)} fusion(bf16[2048,768]{1,0:T(8,128)(2,1)S(1)} %bitcast.223, bf16[768,1152]{1,0:T(8,128)(2,1)S(1)} %bitcast.272, f32[1152]{0:T(1024)S(1)} %add.222), kind=kOutput, calls=%fused_computation.12 | convolution fusion | flops 3628597248 | bytes 9638400 | tf_op jit(solution)/shard_map/dot_general | solution.py:549
  91.9 70.4 %attend_forward.1 = (bf16[2048,384]{1,0:T(8,128)(2,1)}, f32[3,2,2048]{2,1,0:T(2,128)}) custom-call(s32[8]{0:T(128)} %and_select_fusion.low_ref, bf16[2048,1152]{1,0:T(8,128)(2,1)} %add_convert_fusion.q_ref.k_ref.v_ref, bf16[2048,1152]{1,0:T(8,128)(2,1)} %add_convert_fusion.q_ref.k_ref.v_ref, bf16[2048,1152]{1,0:T(8,128)(2,1)} %add_convert_fusion.q_ref.k_ref.v_ref, ...), custom_call_target="tpu_custom_call" | custom-call | flops 3221225472 | bytes 7077888 | tf_op jit(solution)/shard_map/attend_forward/pallas_call | solution.py:107
  162.3 2.1 dynamic-slice_bitcast_fusion.4
  165.6 2.1 dynamic-slice_bitcast_fusion.2
  168.4 1.3 constant_dynamic-slice_fusion.4
  169.7 1.4 bitcast_select_fusion.7
  172.4 14.7 %collective-permute-done.2 = bf16[512,768]{1,0:T(8,128)(2,1)} collective-permute-done((bf16[512,768]{1,0:T(8,128)(2,1)}, bf16[512,768]{1,0:T(8,128)(2,1)}, u32[]{:S(2)}, u32[]{:S(2)}) %collective-permute-start.2) | collective-permute-done | bytes 786464 | tf_op jit(solution)/shard_map/ppermute | solution.py:470
  189.5 1.7 convert_reduce_fusion.4
  191.2 2.6 slice.326
  193.9 4.8 %fusion.50 = (bf16[32,24,768]{2,1,0:T(8,128)(2,1)S(1)}, bf16[32,24,768]{2,1,0:T(8,128)(2,1)S(1)}, bf16[32,24,768]{2,1,0:T(8,128)(2,1)S(1)}, bf16[32,24,768]{2,1,0:T(8,128)(2,1)S(1)}, bf16[32,24,768]{2,1,0:T(8,128)(2,1)S(1)}) fusion(bf16[32,216,768]{2,1,0:T(8,128)(2,1)} %bitcast.213), kind=kLoop, calls=%fused_computation.201 | loop fusion | bytes 11796480 | tf_op jit(solution)/shard_map/slice | solution.py:522
  199.2 1.6 fusion.57
  201.4 9.7 %fusion.25 = f32[1024,3072]{1,0:T(8,128)} fusion(bf16[768,768]{1,0:T(8,128)(2,1)S(1)} %bitcast.239, bf16[768,768]{1,0:T(8,128)(2,1)S(1)} %bitcast.241, bf16[768,768]{1,0:T(8,128)(2,1)S(1)} %bitcast.243, bf16[768,768]{1,0:T(8,128)(2,1)S(1)} %bitcast.237, f32[1024,768]{1,0:T(8,128)S(1)} %get-tuple-element.126, f32[768]{0:T(1024)S(1)} %add.231, ...), kind=kOutput, calls=%fused_computation.71 | convolution fusion | flops 4854644736 | bytes 20461568 | tf_op jit(solution)/shard_map/dot_general | solution.py:565
  211.1 16.4 %convert_reduce_fusion = (f32[3072]{0:T(1024)S(1)}, bf16[1024,3072]{1,0:T(8,128)(2,1)}) fusion(f32[1024,3072]{1,0:T(8,128)} %fusion.25, f32[3072]{0:T(1024)S(1)} %add.234, bf16[1024,768]{1,0:T(8,128)(2,1)S(1)} %bitcast.230, bf16[3072,768]{1,0:T(8,128)(2,1)S(1)} %bitcast.220), kind=kOutput, calls=%fused_computation.9 | convolution fusion | flops 4904186880 | bytes 25190400 | tf_op jit(solution)/shard_map/dot_general | solution.py:26
  227.6 8.7 %multiply_reduce_fusion.1 = (f32[768]{0:T(1024)S(1)}, f32[1024]{0:T(1024)S(1)}, f32[768]{0:T(1024)S(1)}, f32[1024,768]{1,0:T(8,128)S(1)}) fusion(f32[1024,768]{1,0:T(8,128)S(1)} %get-tuple-element.126, f32[1024]{0:T(1024)S(1)} %fusion.35, f32[1024]{0:T(1024)S(1)} %broadcast_multiply_fusion.2, f32[768]{0:T(1024)S(1)} %mul.294, ...), kind=kOutput, calls=%fused_computation.52 | convolution fusion | flops 4857000960 | bytes 17323008 | tf_op jit(solution)/shard_map/dot_general | solution.py:26
  236.3 8.5 %convolution_convert_fusion.1 = bf16[768,3072]{1,0:T(8,128)(2,1)S(1)} fusion(bf16[1024,3072]{1,0:T(8,128)(2,1)} %get-tuple-element.129, f32[1024,768]{1,0:T(8,128)S(1)} %get-tuple-element.126, f32[768]{0:T(1024)S(1)} %add.231, f32[768]{0:T(1024)S(1)} %mul.294, f32[1024]{0:T(1024)S(1)} %fusion.35, f32[1024]{0:T(1024)S(1)} %broadcast_multiply_fusion.2), kind=kOutput, calls=%fused_computation.22 | convolution fusion | flops 4838129664 | bytes 14170112 | tf_op jit(solution)/shard_map/dot_general | solution.py:22
  244.9 1.5 fusion.49
  246.4 1.9 convert_reduce_fusion.5
  248.4 2.5 convolution_convert_fusion.5
  250.9 2.6 convolution_convert_fusion.4
  253.5 2.2 fusion.51
  255.8 9.5 %convolution_convert_fusion = bf16[3072,768]{1,0:T(8,128)(2,1)} fusion(bf16[1024,768]{1,0:T(8,128)(2,1)S(1)} %get-tuple-element.74, f32[1024,3072]{1,0:T(8,128)S(1)} %bitcast.274, f32[3072]{0:T(1024)S(1)} %add.234), kind=kOutput, calls=%fused_computation.21 | convolution fusion | flops 4865654784 | bytes 18886656 | tf_op jit(solution)/shard_map/dot_general | solution.py:22
  265.3 4.5 reshape.475
  269.8 5.2 %constant_dynamic-slice_fusion.1 = (bf16[2,512,1,384]{3,2,1,0:T(2,128)(2,1)S(1)}, bf16[2,512,1,384]{3,2,1,0:T(2,128)(2,1)S(1)}) fusion(bf16[2,512,2,384]{3,2,1,0:T(2,128)(2,1)} %reshape.475, s32[]{:T(128)S(6)} %select_n.174, s32[]{:T(128)S(6)} %select_n.178), kind=kLoop, calls=%fused_computation.160 | loop fusion | bytes 3145736 | tf_op jit(solution)/shard_map/jit(dynamic_index_in_dim)/dynamic_slice | solution.py:595
  281.7 2.5 constant_dynamic-update-slice_fusion.24
  284.7 1.3 copy.45
  287.3 2.4 fusion.10
  290.0 13.3 %multiply_convert_fusion.4 = bf16[1024,768]{1,0:T(8,128)(2,1)S(1)} fusion(f32[1024,768]{1,0:T(8,128)} %copy-done.7, bf16[3072,768]{1,0:T(8,128)(2,1)} %bitcast.221, f32[1024]{0:T(1024)S(1)} %bitcast.255, f32[768]{0:T(1024)S(1)} %add.239, f32[1024,3072]{1,0:T(8,128)} %fusion.25, f32[3072]{0:T(1024)S(1)} %add.234), kind=kOutput, calls=%fused_computation.59 | convolution fusion | flops 4867227648 | bytes 22039552 | tf_op jit(solution)/shard_map/dot_general | solution.py:568
  305.5 67.5 %attend_backward.1 = bf16[2048,1152]{1,0:T(8,128)(2,1)} custom-call(s32[8]{0:T(128)} %convert_reduce_fusion.7.high_ref, bf16[2048,1152]{1,0:T(8,128)(2,1)} %add_convert_fusion.q_ref.k_ref.v_ref, bf16[2048,1152]{1,0:T(8,128)(2,1)} %add_convert_fusion.q_ref.k_ref.v_ref, bf16[2048,1152]{1,0:T(8,128)(2,1)} %add_convert_fusion.q_ref.k_ref.v_ref, ...), custom_call_target="tpu_custom_call" | custom-call | flops 8053063680 | bytes 14155776 | tf_op jit(solution)/shard_map/attend_backward/pallas_call | solution.py:200
  373.0 9.1 %convolution_convert_fusion.2 = bf16[2048,768]{1,0:T(8,128)(2,1)} fusion(bf16[2048,1152]{1,0:T(8,128)(2,1)} %attend_backward.1, bf16[768,1152]{1,0:T(8,128)(2,1)} %bitcast.271), kind=kOutput, calls=%fused_computation.27 | convolution fusion | flops 3625451520 | bytes 9633792 | tf_op jit(solution)/shard_map/dot_general | solution.py:26
  382.8 2.7 dynamic-slice_bitcast_fusion
  386.3 1.6 fusion.30
  387.9 1.3 pad_maximum_fusion.2
  389.2 8.1 %convolution_convert_fusion.3 = bf16[768,1152]{1,0:T(8,128)(2,1)} fusion(bf16[2048,768]{1,0:T(8,128)(2,1)S(1)} %copy-done.17, bf16[2048,1152]{1,0:T(8,128)(2,1)} %attend_backward.1), kind=kOutput, calls=%fused_computation.28 | convolution fusion | flops 3624763392 | bytes 9633792 | tf_op jit(solution)/shard_map/dot_general | solution.py:22
  397.3 2.8 fusion.22
  400.1 1.6 copy-done.2
  401.7 1.6 fusion.21
  404.3 4.3 fusion.13
  409.9 40.7 %reduce_last.1 = (f32[24,1152]{1,0:T(8,128)}, f32[24,1152]{1,0:T(8,128)}, f32[8,128]{1,0:T(8,128)}) custom-call(bf16[4,2,2,48,1152]{4,3,2,1,0:T(8,128)(2,1)} %bitcast.226, f32[4,2,2,8,128]{4,3,2,1,0:T(8,128)} %bitcast.250), custom_call_target="tpu_custom_call" | custom-call | tf_op jit(solution)/shard_map/reduce_last/pallas_call | solution.py:415
  451.7 1.3 dynamic_slice.97
  454.3 1.5 fusion.55
  455.8 1.3 fusion.26
  457.1 1.3 pad_maximum_fusion.5
  458.4 1.5 fusion.52
  460.6 1.6 slice.357
  (203 shorter events, 43.3 us)
Async XLA Ops:
  7.2 184.0 %all-gather.2.cloned.1.call-start = ((), (), s32[]{:S(2)}) async-start(), calls=%async_computation.1 | async-start | bytes 10948608 | tf_op jit(solution)/shard_map/all_gather | solution.py:431
  12.0 0.7 copy-start.27
  12.8 445.7 %reduce-scatter.2.cloned.1.call-start = ((), (), s32[]{:S(2)}) async-start(), calls=%async_computation.2 | async-start | bytes 10948608 | tf_op jit(solution)/shard_map/reduce_scatter | solution.py:435
  13.8 70.7 %copy-start.28 = (s32[2048]{0:T(1024)}, s32[2048]{0:T(1024)S(1)}, u32[]{:S(2)}) copy-start(s32[2048]{0:T(1024)S(1)} %get-tuple-element.47) | copy-start | bytes 24580
  78.6 4.8 %copy-start = (bf16[2,2,512,768]{3,2,1,0:T(8,128)(2,1)S(1)}, bf16[2,2,512,768]{3,2,1,0:T(8,128)(2,1)}, u32[]{:S(2)}) copy-start(bf16[2,2,512,768]{3,2,1,0:T(8,128)(2,1)} %get-tuple-element.24) | copy-start | bytes 9437188
  84.5 1.5 copy-start.30
  164.4 5.3 %collective-permute-start = (bf16[2,512,384]{2,1,0:T(8,128)(2,1)}, bf16[2,512,384]{2,1,0:T(8,128)(2,1)}, u32[]{:S(2)}, u32[]{:S(2)}) collective-permute-start(bf16[2,512,384]{2,1,0:T(8,128)(2,1)} %dynamic-slice_bitcast_fusion.4), channel_id=1, source_target_pairs={{0,1},{1,0},{2,3},{3,2},{4,5},{5,4},{6,7},{7,6},{8,9},{9,8},{10,11... | collective-permute-start | bytes 2359304 | tf_op jit(solution)/shard_map/ppermute | solution.py:554
  167.7 19.4 %collective-permute-start.2 = (bf16[512,768]{1,0:T(8,128)(2,1)}, bf16[512,768]{1,0:T(8,128)(2,1)}, u32[]{:S(2)}, u32[]{:S(2)}) collective-permute-start(bf16[512,768]{1,0:T(8,128)(2,1)} %dynamic-slice_bitcast_fusion.2), channel_id=1, source_target_pairs={{0,2},{1,3},{2,0},{3,1},{4,6},{5,7},{6,4},{7,5},{8,10},{9,11},{10,... | collective-permute-start | bytes 2359304 | tf_op jit(solution)/shard_map/ppermute | solution.py:470
  168.1 1.6 copy-start.22
  169.7 17.4 %copy-start.21 = (bf16[2,512,768]{2,1,0:T(8,128)(2,1)S(1)}, bf16[2,512,768]{2,1,0:T(8,128)(2,1)}, u32[]{:S(2)}) copy-start(bf16[2,512,768]{2,1,0:T(8,128)(2,1)} %param.16) | copy-start | bytes 4718596
  188.3 0.9 copy-start.3
  188.4 1.1 copy-start.5
  193.8 17.3 %copy-start.14 = (bf16[32,96,768]{2,1,0:T(8,128)(2,1)}, bf16[32,96,768]{2,1,0:T(8,128)(2,1)S(1)}, u32[]{:S(2)}) copy-start(bf16[32,96,768]{2,1,0:T(8,128)(2,1)S(1)} %slice.326) | copy-start | bytes 14155780
  193.8 4.9 %copy-start.19 = (bf16[2,512,768]{2,1,0:T(8,128)(2,1)S(1)}, bf16[2,512,768]{2,1,0:T(8,128)(2,1)}, u32[]{:S(2)}) copy-start(bf16[2,512,768]{2,1,0:T(8,128)(2,1)} %pad_maximum_fusion.1) | copy-start | bytes 4718596
  193.9 5.3 %copy-start.24 = (bf16[2,1,512,768]{3,2,1,0:T(8,128)(2,1)S(1)}, bf16[2,1,512,768]{3,2,1,0:T(8,128)(2,1)}, u32[]{:S(2)}) copy-start(bf16[2,1,512,768]{3,2,1,0:T(8,128)(2,1)} %constant_dynamic-slice_fusion.4) | copy-start | bytes 4718596
  198.7 2.7 copy-start.25
  200.8 44.0 %copy-start.7 = (f32[1024,768]{1,0:T(8,128)}, f32[1024,768]{1,0:T(8,128)S(1)}, u32[]{:S(2)}) copy-start(f32[1024,768]{1,0:T(8,128)S(1)} %get-tuple-element.126) | copy-start | bytes 9437188
  201.4 9.8 %copy-start.20 = (bf16[2,512,768]{2,1,0:T(8,128)(2,1)S(1)}, bf16[2,512,768]{2,1,0:T(8,128)(2,1)}, u32[]{:S(2)}) copy-start(bf16[2,512,768]{2,1,0:T(8,128)(2,1)} %get-tuple-element.49) | copy-start | bytes 4718596
  244.9 1.6 copy-start.4
  244.9 1.6 copy-start.6
  246.4 2.0 copy-start.1
  248.4 7.3 %slice-start = ((s8[12582912]{0:T(1024)(128)(4,1)}), s8[4194304]{0:T(1024)(128)(4,1)S(1)}, s32[]{:S(2)}) async-start(s8[12582912]{0:T(1024)(128)(4,1)} %bitcast.273), calls=%async_computation.3 | async-start | bytes 8388608
  250.9 4.8 %slice-start.1 = ((s8[12582912]{0:T(1024)(128)(4,1)}), s8[4194304]{0:T(1024)(128)(4,1)S(1)}, s32[]{:S(2)}) async-start(s8[12582912]{0:T(1024)(128)(4,1)} %bitcast.273), calls=%async_computation.4 | async-start | bytes 8388608
  250.9 4.8 %slice-start.2 = ((s8[12582912]{0:T(1024)(128)(4,1)}), s8[4194304]{0:T(1024)(128)(4,1)S(1)}, s32[]{:S(2)}) async-start(s8[12582912]{0:T(1024)(128)(4,1)} %bitcast.273), calls=%async_computation.5 | async-start | bytes 8388608
  269.8 6.3 %copy-start.26 = (bf16[768,768]{1,0:T(8,128)(2,1)S(1)}, bf16[768,768]{1,0:T(8,128)(2,1)}, u32[]{:S(2)}) copy-start(bf16[768,768]{1,0:T(8,128)(2,1)} %convolution_convert_fusion.5) | copy-start | bytes 3538948
  275.0 2.1 copy-start.13
  275.0 3.3 copy-start.12
  275.2 9.1 %collective-permute-start.3 = (bf16[2,512,384]{2,1,0:T(8,128)(2,1)S(1)}, bf16[2,512,384]{2,1,0:T(8,128)(2,1)S(1)}, u32[]{:S(2)}, u32[]{:S(2)}) collective-permute-start(bf16[2,512,384]{2,1,0:T(8,128)(2,1)S(1)} %bitcast.246), channel_id=1, source_target_pairs={{0,1},{1,0},{2,3},{3,2},{4,5},{5,4},{6,7},{7,6},{8,9},{9,8},{10,11... | collective-permute-start | bytes 2359304 | tf_op jit(solution)/shard_map/ppermute | solution.py:596
  276.1 3.3 copy-start.11
  277.2 3.4 copy-start.10
  278.3 3.4 copy-start.16
  286.0 0.7 copy-start.31
  303.4 1.1 copy-start.23
  305.4 80.8 %collective-permute-start.1 = (bf16[512,768]{1,0:T(8,128)(2,1)}, bf16[512,768]{1,0:T(8,128)(2,1)}, u32[]{:S(2)}, u32[]{:S(2)}) collective-permute-start(bf16[512,768]{1,0:T(8,128)(2,1)} %dynamic-slice_bitcast_fusion.3), channel_id=1, source_target_pairs={{0,2},{1,3},{2,0},{3,1},{4,6},{5,7},{6,4},{7,5},{8,10},{9,11},{10,... | collective-permute-start | bytes 2359304 | tf_op jit(solution)/shard_map/ppermute | solution.py:476
  373.0 9.1 %copy-start.15 = (bf16[2048,1152]{1,0:T(8,128)(2,1)S(1)}, bf16[2048,1152]{1,0:T(8,128)(2,1)}, u32[]{:S(2)}) copy-start(bf16[2048,1152]{1,0:T(8,128)(2,1)} %attend_backward.1) | copy-start | bytes 14155780
  385.5 11.8 %collective-permute-start.4 = (bf16[2,512,768]{2,1,0:T(8,128)(2,1)}, bf16[2,512,768]{2,1,0:T(8,128)(2,1)}, u32[]{:S(2)}, u32[]{:S(2)}) collective-permute-start(bf16[2,512,768]{2,1,0:T(8,128)(2,1)} %dynamic-slice_bitcast_fusion), channel_id=1, source_target_pairs={{0,1},{1,0},{2,3},{3,2},{4,5},{5,4},{6,7},{7,6},{8,9},{9,8},{10,11... | collective-permute-start | bytes 4718600 | tf_op jit(solution)/shard_map/ppermute | solution.py:607
  386.2 2.9 copy-start.17
  389.2 8.1 %copy-start.18 = (bf16[2048,768]{1,0:T(8,128)(2,1)S(1)}, bf16[2048,768]{1,0:T(8,128)(2,1)}, u32[]{:S(2)}) copy-start(bf16[2048,768]{1,0:T(8,128)(2,1)} %convolution_convert_fusion.2) | copy-start | bytes 9437188
  400.1 1.6 copy-start.2
  408.6 1.1 copy-start.8
  409.8 46.0 %copy-start.9 = (bf16[1024,768]{1,0:T(8,128)(2,1)S(1)}, bf16[1024,768]{1,0:T(8,128)(2,1)}, u32[]{:S(2)}) copy-start(bf16[1024,768]{1,0:T(8,128)(2,1)} %copy-done.8) | copy-start | bytes 4718596
  409.8 46.0 %collective-permute-start.5 = (bf16[512,768]{1,0:T(8,128)(2,1)S(1)}, bf16[512,768]{1,0:T(8,128)(2,1)}, u32[]{:S(2)}, u32[]{:S(2)}) collective-permute-start(bf16[512,768]{1,0:T(8,128)(2,1)S(1)} %dynamic-slice_bitcast_fusion.1), channel_id=1, source_target_pairs={{0,2},{1,3},{2,0},{3,1},{4,6},{5,7},{6,4},{7,5},{8,10},{9,11},{10,... | collective-permute-start | bytes 2359304 | tf_op jit(solution)/shard_map/ppermute | solution.py:476
  455.8 2.6 copy-start.29
Sparse Core Ops, SparseCore 0:
  12.9 100.1 all-gather.1
  286.2 144.8 reduce-scatter.1

commit v2 on v1

--- a/solution.py
+++ b/solution.py
@@ -42,6 +42,11 @@
     return jnp.where(lane < HD, rows, nothing), jnp.where(lane < HD, nothing, rows)
 
 
+def third(packed, part, g):
+    first = part * (packed.shape[1] // 3) + g * PAIR
+    return slice(first, first + PAIR)
+
+
 def allowed_in(key_block, row_block, begins, diagonal):
     keys = key_block * TILE + lax.broadcasted_iota(jnp.int32, (TILE, TILE), 0)
     allowed = keys >= begins
@@ -51,49 +56,61 @@
     return allowed
 
 
-def attend_kernel(low_ref, q_ref, k_ref, v_ref, begin_ref, out_ref, logsum_ref, value_t):
-    blocks = q_ref.shape[0] // TILE
-    for block in range(blocks):
-        at = slice(block * TILE, (block + 1) * TILE)
-        value_t[:, at] = v_ref[at, :].T
+def attend_kernel(bounds_ref, packed_ref, begin_ref, out_ref, logsum_ref, value_t, held):
+    blocks = packed_ref.shape[0] // TILE
+    groups = out_ref.shape[1] // PAIR
+    count = 2 * groups
+    for g in range(groups):
+        for block in range(blocks):
+            at = slice(block * TILE, (block + 1) * TILE)
+            value_t[g * PAIR : (g + 1) * PAIR, at] = packed_ref[at, third(packed_ref, 2, g)].T
 
     def one_row_block(i, carry):
         here = pl.ds(pl.multiple_of(i * TILE, TILE), TILE)
-        heads = split_pair(q_ref[here, :] * HD ** (-0.5))
         begins = begin_ref[:, here]
-
-        def visit(j, state, diagonal):
+        heads = []
+        for g in range(groups):
+            heads += split_pair(packed_ref[here, third(packed_ref, 0, g)] * HD ** (-0.5))
+
+        def score(j, tops, masked, diagonal):
             there = pl.ds(pl.multiple_of(j * TILE, TILE), TILE)
-            key_rows = k_ref[there, :]
-            allowed = allowed_in(j, i, begins, diagonal)
+            allowed = allowed_in(j, i, begins, diagonal) if masked else None
+            new_tops = []
+            for h in range(count):
+                g = h // 2
+                key_rows = packed_ref[there, third(packed_ref, 1, g)]
+                scores = against_rows(key_rows, heads[h])
+                if masked:
+                    scores = jnp.where(allowed, scores, MASKED)
+                held[h, there, :] = scores
+                top = jnp.max(scores, axis=0, keepdims=True)
+                new_tops.append(top if tops is None else jnp.maximum(top, tops[h]))
+            return tuple(new_tops)
+
+        tops = score(i, None, True, True)
+        tops = lax.fori_loop(bounds_ref[0, i], bounds_ref[1, i], lambda j, s: score(j, s, True, False), tops)
+        tops = lax.fori_loop(bounds_ref[1, i], i, lambda j, s: score(j, s, False, False), tops)
+
+        def mix(j, state):
+            there = pl.ds(pl.multiple_of(j * TILE, TILE), TILE)
             new_state = []
-            for which in range(2):
-                scores = against_rows(key_rows, heads[which])
-                scores = jnp.where(allowed, scores, MASKED)
-                top = jnp.max(scores, axis=0, keepdims=True)
-                if state is not None:
-                    old_top, old_total, old_mix = state[which]
-                    top = jnp.maximum(top, old_top)
-                weights = jnp.exp(scores - top)
-                total = jnp.sum(weights, axis=0, keepdims=True)
-                mix = jnp.dot(
-                    value_t[which * HD : (which + 1) * HD, there],
-                    weights.astype(BF16),
-                    preferred_element_type=F32,
+            for h in range(count):
+                weights = jnp.exp(held[h, there, :] - tops[h])
+                total, mixed = state[h]
+                total = total + jnp.sum(weights, axis=0, keepdims=True)
+                mixed = mixed + jnp.dot(
+                    value_t[h * HD : (h + 1) * HD, there], weights.astype(BF16), preferred_element_type=F32
                 )
-                if state is not None:
-                    fade = jnp.exp(old_top - top)
-                    total = total + fade * old_total
-                    mix = mix + fade * old_mix
-                new_state.append((top, total, mix))
+                new_state.append((total, mixed))
             return tuple(new_state)
 
-        state = visit(i, None, True)
-        state = lax.fori_loop(low_ref[i], i, lambda j, s: visit(j, s, False), state)
-        mixed = [mix / total for _, total, mix in state]
-        out_ref[here, :] = jnp.concatenate(mixed, axis=0).T.astype(BF16)
-        logs = [top + jnp.log(total) for top, total, _ in state]
-        logsum_ref[0, :, here] = jnp.concatenate(logs, axis=0)
+        empty = (jnp.zeros((1, TILE), F32), jnp.zeros((HD, TILE), F32))
+        state = lax.fori_loop(bounds_ref[0, i], i + 1, mix, (empty,) * count)
+        for g in range(groups):
+            mixed = [mix / total for total, mix in state[2 * g : 2 * g + 2]]
+            out_ref[here, g * PAIR : (g + 1) * PAIR] = jnp.concatenate(mixed, axis=0).T.astype(BF16)
+        logs = [top + jnp.log(total) for top, (total, _) in zip(tops, state)]
+        logsum_ref[:, here] = jnp.concatenate(logs, axis=0)
         return carry
 
     lax.fori_loop(0, blocks, one_row_block, 0)
@@ -102,122 +119,134 @@
 def attend_forward(packed, low_blocks, begins):
     bucket, columns = packed.shape
     groups = columns // 3 // PAIR
-    tall = lambda part: pl.BlockSpec((bucket, PAIR), lambda g, low: (0, 3 * g + part))
-    narrow = pl.BlockSpec((bucket, PAIR), lambda g, low: (0, g))
     return pl.pallas_call(
         attend_kernel,
         name="attend_forward",
         out_shape=(
             jax.ShapeDtypeStruct((bucket, columns // 3), BF16),
-            jax.ShapeDtypeStruct((groups, 2, bucket), F32),
+            jax.ShapeDtypeStruct((2 * groups, bucket), F32),
         ),
         grid_spec=pltpu.PrefetchScalarGridSpec(
             num_scalar_prefetch=1,
-            grid=(groups,),
+            grid=(1,),
             in_specs=[
-                tall(0),
-                tall(1),
-                tall(2),
+                pl.BlockSpec((bucket, columns), lambda g, low: (0, 0)),
                 pl.BlockSpec((1, bucket), lambda g, low: (0, 0)),
             ],
-            out_specs=[narrow, pl.BlockSpec((1, 2, bucket), lambda g, low: (g, 0, 0))],
-            scratch_shapes=[pltpu.VMEM((PAIR, bucket), BF16)],
+            out_specs=[
+                pl.BlockSpec((bucket, columns // 3), lambda g, low: (0, 0)),
+                pl.BlockSpec((2 * groups, bucket), lambda g, low: (0, 0)),
+            ],
+            scratch_shapes=[
+                pltpu.VMEM((groups * PAIR, bucket), BF16),
+                pltpu.VMEM((2 * groups, bucket, TILE), F32),
+            ],
         ),
         cost_estimate=pl.CostEstimate(
             flops=4 * 2 * groups * bucket * bucket * HD // 2,
             bytes_accessed=bucket * columns * 3,
             transcendentals=2 * groups * bucket * bucket // 2,
         ),
-    )(low_blocks, packed, packed, packed, begins)
+    )(low_blocks, packed, begins)
 
 
 def attend_back_kernel(
-    high_ref, q_ref, k_ref, v_ref, o_ref, go_ref, begin_ref, logsum_ref, out_ref, key_t, query_t, delta
+    bounds_ref, packed_ref, o_ref, go_ref, begin_ref, logsum_ref, out_ref, key_t, query_t, delta
 ):
-    blocks = q_ref.shape[0] // TILE
+    blocks = packed_ref.shape[0] // TILE
+    groups = o_ref.shape[1] // PAIR
     half = lax.broadcasted_iota(jnp.int32, (8, PAIR), 1) // HD
     picks = (half == lax.broadcasted_iota(jnp.int32, (8, PAIR), 0)).astype(F32)
-    for block in range(blocks):
-        at = slice(block * TILE, (block + 1) * TILE)
-        key_t[:, at] = k_ref[at, :].T
-        query_t[:, at] = jnp.zeros((PAIR, TILE), F32)
-        product = o_ref[at, :].astype(F32) * go_ref[at, :].astype(F32)
-        delta[:, at] = lax.dot_general(
-            picks,
-            product,
-            (((1,), (1,)), ((), ())),
-            precision=lax.Precision.HIGHEST,
-            preferred_element_type=F32,
-        )
+    for g in range(groups):
+        column = slice(g * PAIR, (g + 1) * PAIR)
+        for block in range(blocks):
+            at = slice(block * TILE, (block + 1) * TILE)
+            key_t[column, at] = packed_ref[at, third(packed_ref, 1, g)].T
+            query_t[column, at] = jnp.zeros((PAIR, TILE), F32)
+            product = o_ref[at, column].astype(F32) * go_ref[at, column].astype(F32)
+            delta[g * 8 : (g + 1) * 8, at] = lax.dot_general(
+                picks,
+                product,
+                (((1,), (1,)), ((), ())),
+                precision=lax.Precision.HIGHEST,
+                preferred_element_type=F32,
+            )
 
     def one_key_block(j, carry):
         there = pl.ds(pl.multiple_of(j * TILE, TILE), TILE)
-        key_rows = k_ref[there, :]
-        value_rows = v_ref[there, :]
-
-        def visit(i, state, diagonal):
+
+        def visit(i, state, masked, diagonal):
             here = pl.ds(pl.multiple_of(i * TILE, TILE), TILE)
-            queries = split_pair(q_ref[here, :] * HD ** (-0.5))
-            grads = split_pair(go_ref[here, :])
-            allowed = allowed_in(j, i, begin_ref[:, here], diagonal)
-            key_grad, value_grad = state
-            for which in range(2):
-                scores = against_rows(key_rows, queries[which])
-                scores = jnp.where(allowed, scores, MASKED)
-                probs = jnp.exp(scores - logsum_ref[0, which : which + 1, here])
-                grad_probs = against_rows(value_rows, grads[which])
-                grad_scores = (probs * (grad_probs - delta[which : which + 1, here])).astype(BF16)
-                value_grad = value_grad + jnp.dot(
-                    probs.astype(BF16), grads[which], preferred_element_type=F32
-                )
-                key_grad = key_grad + jnp.dot(
-                    grad_scores, queries[which], preferred_element_type=F32
-                )
-                at = slice(which * HD, (which + 1) * HD)
-                query_t[at, here] += jnp.dot(
-                    key_t[at, there], grad_scores, preferred_element_type=F32
-                )
-            return key_grad, value_grad
+            allowed = allowed_in(j, i, begin_ref[:, here], diagonal) if masked else None
+            new_state = []
+            for g in range(groups):
+                key_rows = packed_ref[there, third(packed_ref, 1, g)]
+                value_rows = packed_ref[there, third(packed_ref, 2, g)]
+                queries = split_pair(packed_ref[here, third(packed_ref, 0, g)] * HD ** (-0.5))
+                grads = split_pair(go_ref[here, g * PAIR : (g + 1) * PAIR])
+                key_grad, value_grad = state[g]
+                for which in range(2):
+                    h = 2 * g + which
+                    scores = against_rows(key_rows, queries[which])
+                    if masked:
+                        scores = jnp.where(allowed, scores, MASKED)
+                    probs = jnp.exp(scores - logsum_ref[h : h + 1, here])
+                    grad_probs = against_rows(value_rows, grads[which])
+                    row = 8 * g + which
+                    grad_scores = (probs * (grad_probs - delta[row : row + 1, here])).astype(BF16)
+                    value_grad = value_grad + jnp.dot(
+                        probs.astype(BF16), grads[which], preferred_element_type=F32
+                    )
+                    key_grad = key_grad + jnp.dot(
+                        grad_scores, queries[which], preferred_element_type=F32
+                    )
+                    at = slice(h * HD, (h + 1) * HD)
+                    query_t[at, here] += jnp.dot(
+                        key_t[at, there], grad_scores, preferred_element_type=F32
+                    )
+                new_state.append((key_grad, value_grad))
+            return tuple(new_state)
 
         zero = jnp.zeros((TILE, PAIR), F32)
-        state = visit(j, (zero, zero), True)
-        state = lax.fori_loop(j + 1, high_ref[j], lambda i, s: visit(i, s, False), state)
-        out_ref[there, PAIR : 2 * PAIR] = state[0].astype(BF16)
-        out_ref[there, 2 * PAIR :] = state[1].astype(BF16)
+        state = visit(j, ((zero, zero),) * groups, True, True)
+        state = lax.fori_loop(j + 1, bounds_ref[1, j], lambda i, s: visit(i, s, False, False), state)
+        state = lax.fori_loop(bounds_ref[1, j], bounds_ref[0, j], lambda i, s: visit(i, s, True, False), state)
+        for g in range(groups):
+            out_ref[there, third(packed_ref, 1, g)] = state[g][0].astype(BF16)
+            out_ref[there, third(packed_ref, 2, g)] = state[g][1].astype(BF16)
         return carry
 
     lax.fori_loop(0, blocks, one_key_block, 0)
-    for block in range(blocks):
-        at = slice(block * TILE, (block + 1) * TILE)
-        out_ref[at, :PAIR] = (query_t[:, at].T * HD ** (-0.5)).astype(BF16)
+    for g in range(groups):
+        for block in range(blocks):
+            at = slice(block * TILE, (block + 1) * TILE)
+            rows = query_t[g * PAIR : (g + 1) * PAIR, at].T * HD ** (-0.5)
+            out_ref[at, third(packed_ref, 0, g)] = rows.astype(BF16)
 
 
 def attend_backward(packed, attended, grad_attended, logsum, high_blocks, begins):
     bucket, columns = packed.shape
     groups = columns // 3 // PAIR
-    tall = lambda part: pl.BlockSpec((bucket, PAIR), lambda g, high: (0, 3 * g + part))
-    narrow = pl.BlockSpec((bucket, PAIR), lambda g, high: (0, g))
+    whole = lambda rows, width: pl.BlockSpec((rows, width), lambda g, high: (0, 0))
     return pl.pallas_call(
         attend_back_kernel,
         name="attend_backward",
         out_shape=jax.ShapeDtypeStruct((bucket, columns), BF16),
         grid_spec=pltpu.PrefetchScalarGridSpec(
             num_scalar_prefetch=1,
-            grid=(groups,),
+            grid=(1,),
             in_specs=[
-                tall(0),
-                tall(1),
-                tall(2),
-                narrow,
-                narrow,
-                pl.BlockSpec((1, bucket), lambda g, high: (0, 0)),
-                pl.BlockSpec((1, 2, bucket), lambda g, high: (g, 0, 0)),
+                whole(bucket, columns),
+                whole(bucket, columns // 3),
+                whole(bucket, columns // 3),
+                whole(1, bucket),
+                whole(2 * groups, bucket),
             ],
-            out_specs=pl.BlockSpec((bucket, 3 * PAIR), lambda g, high: (0, g)),
+            out_specs=whole(bucket, columns),
             scratch_shapes=[
-                pltpu.VMEM((PAIR, bucket), BF16),
-                pltpu.VMEM((PAIR, bucket), F32),
-                pltpu.VMEM((8, bucket), F32),
+                pltpu.VMEM((groups * PAIR, bucket), BF16),
+                pltpu.VMEM((groups * PAIR, bucket), F32),
+                pltpu.VMEM((groups * 8, bucket), F32),
             ],
         ),
         cost_estimate=pl.CostEstimate(
@@ -225,7 +254,7 @@
             bytes_accessed=bucket * columns * 6,
             transcendentals=2 * groups * bucket * bucket // 2,
         ),
-    )(high_blocks, packed, packed, packed, attended, grad_attended, begins, logsum)
+    )(high_blocks, packed, attended, grad_attended, begins, logsum)
 
 
 def position():
@@ -260,30 +289,42 @@
     pl.semaphore_wait(barrier, len(others))
 
 
-def gather_kernel(token_ref, half_ref, tiny_ref, all_tokens, all_half, all_tiny, local_sem, *semaphores):
+def gather_kernel(
+    token_ref, cotangent_ref, weight_ref, tiny_ref, all_tokens, all_cotangent, all_half, all_tiny, local_sem, *semaphores
+):
     z, x, y, core = position()
     token_sems, half_sems, tiny_sems = [semaphores[2 * i : 2 * i + 2] for i in range(3)]
     meet(z, x, y, core)
     core_twin, y_twin, x_twin = device(z, x, y, 1 - core), device(z, x, 1 - y, core), device(z, 1 - x, y, core)
-    streams = [
-        (half_ref.at[core], half_ref.at[1 - core], all_half, half_sems),
-        (tiny_ref, tiny_ref, all_tiny, tiny_sems),
+    columns = all_half.shape[5] // 3
+
+    def weight_part(part, c):
+        first = pl.multiple_of(part * 2 * columns + c * columns, PAIR)
+        return weight_ref.at[:, pl.ds(first, columns)]
+
+    streams = [(all_half, half_sems), (all_tiny, tiny_sems)]
+    sent = []
+    local = [
+        pltpu.make_async_copy(token_ref.at[y], all_tokens.at[y, core], local_sem.at[0]),
+        pltpu.make_async_copy(cotangent_ref.at[y], all_cotangent.at[y], local_sem.at[1]),
+        pltpu.make_async_copy(tiny_ref, all_tiny.at[z, x, y, core], local_sem.at[2]),
     ]
-    sent = []
-    local = [pltpu.make_async_copy(token_ref.at[y], all_tokens.at[y, core], local_sem.at[2])]
-    for i, (mine, _, whole, _) in enumerate(streams):
-        local.append(pltpu.make_async_copy(mine, whole.at[z, x, y, core], local_sem.at[i]))
-    for copy in local:
+    swaps = [send(tiny_ref, all_tiny.at[z, x, y, core], tiny_sems, 0, core_twin)]
+    for part in range(3):
+        mine = all_half.at[z, x, y, core, :, part * columns : (part + 1) * columns]
+        local.append(pltpu.make_async_copy(weight_part(part, core), mine, local_sem.at[3 + part]))
+        swaps.append(send(weight_part(part, 1 - core), mine, half_sems, (0, 16, 17)[part], core_twin))
+    for copy in local[2:] + local[:2]:
         copy.start()
-    swaps = [send(twins, whole.at[z, x, y, core], sems, 0, core_twin) for _, twins, whole, sems in streams]
-    for copy in local[1:]:
+    for copy in local[2:]:
         copy.wait()
     for copy in swaps:
         copy.wait_recv()
     sent += swaps
-    own = [(whole.at[z, x, y], sems) for _, _, whole, sems in streams]
+    own = [(whole.at[z, x, y], sems) for whole, sems in streams]
     over_y = [send(piece, piece, sems, 1, y_twin) for piece, sems in own]
     token_y = send(token_ref.at[1 - y], all_tokens.at[y, core], token_sems, 0, y_twin)
+    cotangent_y = send(cotangent_ref.at[1 - y], all_cotangent.at[y], token_sems, 3, y_twin)
     token_own = send(token_ref.at[y], all_tokens.at[y, core], token_sems, 1, core_twin)
     along_z, over_x = {}, []
 
@@ -297,27 +338,28 @@
     spread_piece(0, own)
     for copy in over_y:
         copy.wait_recv()
-    spread_piece(1, [(whole.at[z, x, 1 - y], sems) for _, _, whole, sems in streams])
+    spread_piece(1, [(whole.at[z, x, 1 - y], sems) for whole, sems in streams])
     token_y.wait_recv()
     token_next = send(all_tokens.at[1 - y, core], all_tokens.at[1 - y, core], token_sems, 2, core_twin)
     for p in (0, 1):
         row = y if p == 0 else 1 - y
         for t in (1, 2, 3):
             source = lax.rem(z + 4 - t, 4)
-            for i, (_, _, whole, sems) in enumerate(streams):
+            for i, (whole, sems) in enumerate(streams):
                 along_z[p, t, i].wait_recv()
                 piece = whole.at[source, x, row]
                 over_x.append(send(piece, piece, sems, 8 + 4 * p + t, x_twin))
-    for copy in over_x + [token_own, token_next]:
+    for copy in over_x + [token_own, token_next, cotangent_y]:
         copy.wait_recv()
-    for copy in sent + over_y + [token_y, token_own, token_next] + list(along_z.values()) + over_x:
+    for copy in sent + over_y + [token_y, token_own, token_next, cotangent_y] + list(along_z.values()) + over_x:
         copy.wait_send()
     local[0].wait()
-
-
-def gather_first(tokens, half_shard, tiny_shard):
+    local[1].wait()
+
+
+def gather_first(tokens, cotangent, weight, tiny):
     _, local_rows, width = tokens.shape
-    _, rows, half_columns = half_shard.shape
+    rows, columns = weight.shape
     anywhere = pl.BlockSpec(memory_space=pl.ANY)
     near = pl.BlockSpec(memory_space=pltpu.VMEM)
     sems = pltpu.SemaphoreType.DMA
@@ -326,14 +368,15 @@
         name="gather_first",
         out_shape=(
             jax.ShapeDtypeStruct((2, 2, local_rows, width), BF16),
-            jax.ShapeDtypeStruct((4, 2, 2, 2, rows, half_columns), BF16),
+            jax.ShapeDtypeStruct((2, local_rows, width), BF16),
+            jax.ShapeDtypeStruct((4, 2, 2, 2, rows, columns // 2), BF16),
             jax.ShapeDtypeStruct((4, 2, 2, 2, 8, 128), F32),
         ),
-        in_specs=[near, near, near],
-        out_specs=[anywhere, anywhere, anywhere],
-        scratch_shapes=[sems((3,)), sems((3,)), sems((3,)), sems((16,)), sems((16,)), sems((16,)), sems((16,))],
+        in_specs=[near] * 4,
+        out_specs=[anywhere] * 4,
+        scratch_shapes=[sems((6,)), sems((4,)), sems((4,)), sems((18,)), sems((18,)), sems((16,)), sems((16,))],
         compiler_params=pltpu.CompilerParams(collective_id=1, has_side_effects=True),
-    )(tokens, half_shard, tiny_shard)
+    )(tokens, cotangent, weight, tiny)
 
 
 def reduce_kernel(big_ref, tiny_ref, own_ref, other_ref, sum_ref, *scratch):
@@ -383,14 +426,14 @@
             three[t, i].wait_recv()
         total_ref[...] += sum(came_three[t].astype(F32) for t in range(3))
         rows = came_last.shape[0]
-        piece = total_ref if i == 1 else total_ref.at[pl.ds(pl.multiple_of((1 - core) * rows, 8), rows)]
+        piece = total_ref.at[pl.ds(pl.multiple_of((1 - core) * rows, 8), rows)]
         last.append(send(piece, came_last, (leave, arrive), 15, device(z, x, y, 1 - core)))
     rows = own_ref.shape[0]
     own_ref[...] = streams[0][6][pl.ds(pl.multiple_of(core * rows, 8), rows)]
     for copy in last:
         copy.wait_recv()
     other_ref[...] = streams[0][7][...]
-    sum_ref[...] = streams[1][6][...] + streams[1][7][...]
+    sum_ref[...] = streams[1][6][pl.ds(pl.multiple_of(core * 8, 8), 8)] + streams[1][7][...]
     for copy in list(one.values()) + list(two.values()) + list(three.values()) + last:
         copy.wait_send()
 
@@ -399,7 +442,7 @@
     rows, half_columns = big.shape[3:]
     near = pl.BlockSpec(memory_space=pltpu.VMEM)
     scratch = []
-    for shape, kind, kept in (((rows, half_columns), BF16, (rows // 2, half_columns)), ((8, 128), F32, (8, 128))):
+    for shape, kind, kept in (((rows, half_columns), BF16, (rows // 2, half_columns)), ((16, 128), F32, (8, 128))):
         scratch += [
             pltpu.VMEM((4, 2) + shape, kind),
             pltpu.VMEM((4, 2) + shape, kind),
@@ -480,52 +523,38 @@
         first, second = jnp.where(core == 0, own, other), jnp.where(core == 0, other, own)
         return jnp.stack([first, second], axis=1).reshape((bucket,) + own.shape[2:])
 
-    own_cotangent = own_micro(cotangent)
 
     vectors = (gain_first, shift_first, packed_bias, output_bias, gain_second, shift_second, expand_bias, reduce_bias)
     sizes = [v.shape[0] for v in vectors]
     small_count = sum(sizes)
     pieces_per_row = hidden_width // width
     rows = output_weight.shape[0]
-    blocks = columns // PAIR
-    tiny = jnp.pad(jnp.concatenate(vectors).astype(F32), (0, 1024 - small_count)).reshape(8, 128)
-    halves = jnp.stack(
-        [
-            jnp.concatenate(
-                [
-                    packed_weight[:, part * width + c * columns + g * PAIR :][:, :PAIR]
-                    for g in range(blocks)
-                    for part in range(3)
-                ],
-                axis=1,
-            )
-            for c in range(share)
-        ]
-    )
+    tiny = jnp.concatenate([jnp.pad(v.astype(F32), (0, 128 - v.shape[0])) for v in vectors]).reshape(8, 128)
     own_kernels = devices == 32 and groups == 4
     if own_kernels:
-        all_tokens, half_packed, all_tiny = gather_first(tokens, halves, tiny)
+        all_tokens, own_cotangent, half_packed, all_tiny = gather_first(tokens, cotangent, packed_weight, tiny)
         everyone = all_tokens.reshape(bucket, width)
         own_tokens = lax.dynamic_index_in_dim(all_tokens, core, 1, keepdims=False)
         half_packed = half_packed.reshape(width, 3 * columns)
     else:
-        own_tokens = own_micro(tokens)
+        own_tokens, own_cotangent = own_micro(tokens), own_micro(cotangent)
         everyone = interleave(own_tokens, lax.ppermute(own_tokens, "seq", swap_core))
-        half_packed = lax.all_gather(halves, ("dp", "seq"), axis=1, tiled=True)
-        half_packed = lax.dynamic_index_in_dim(half_packed, core, 0, keepdims=False)
+        full_packed = gather_rows(packed_weight)
+        half_packed = jnp.concatenate(
+            [lax.dynamic_slice(full_packed, (0, part * width + core * columns), (width, columns)) for part in range(3)], axis=1
+        )
         all_tiny = gather_rows(tiny)
-    small_all = all_tiny.reshape(devices, 1024)
+    small_all = all_tiny.reshape(devices, 8, 128)
     expand_blocks = [expand_weight[:, j * width : (j + 1) * width] for j in range(pieces_per_row)]
-    second = gather_rows(jnp.concatenate([output_weight] + expand_blocks + [reduce_weight])).reshape(devices, -1, width)
+    second_shard = jnp.concatenate([output_weight] + expand_blocks + [reduce_weight])
+    small_all, second_shard = lax.optimization_barrier((small_all, second_shard))
+    second = gather_rows(second_shard).reshape(devices, -1, width)
     full_output = second[:, :rows].reshape(width, width)
     full_expand = jnp.concatenate(
         [second[:, rows * (j + 1) : rows * (j + 2)].reshape(width, width) for j in range(pieces_per_row)], axis=1
     )
     full_reduce = second[:, rows * (pieces_per_row + 1) :].reshape(hidden_width, width)
-    pieces, at = [], 0
-    for size in sizes:
-        pieces.append(small_all[:, at : at + size].reshape(-1))
-        at += size
+    pieces = [small_all[:, i, :size].reshape(-1) for i, size in enumerate(sizes)]
     gain_one, shift_one, packed_shift, output_shift, gain_two, shift_two, expand_shift, reduce_shift = pieces
 
     places = jnp.arange(bucket, dtype=jnp.int32)
@@ -534,9 +563,13 @@
     ends = jnp.cumsum(bucket_lengths)
     past = (places[:, None] >= ends[None, :]).astype(jnp.int32)
     begins = jnp.sum(past * bucket_lengths[None, :], axis=1)
-    low_blocks = begins[::TILE] // TILE
     block_ids = jnp.arange(bucket // TILE, dtype=jnp.int32)
-    high_blocks = jnp.sum((low_blocks[None, :] <= block_ids[:, None]).astype(jnp.int32), axis=1)
+    first_begin, last_begin = begins[::TILE], begins[TILE - 1 :: TILE]
+    low = first_begin // TILE
+    low_blocks = jnp.stack([low, jnp.minimum(-(-last_begin // TILE), block_ids)])
+    high = jnp.sum((low[None, :] <= block_ids[:, None]).astype(jnp.int32), axis=1)
+    free = jnp.sum((last_begin[None, :] <= block_ids[:, None] * TILE).astype(jnp.int32), axis=1)
+    high_blocks = jnp.stack([high, jnp.clip(free, block_ids + 1, high)])
     begins = begins[None, :]
     valid_all = (jnp.sum(past, axis=1) < slot_count - 1).astype(F32).reshape(2, share, local_rows)
     valid = lax.dynamic_index_in_dim(valid_all, core, 1, keepdims=False).reshape(-1, 1)
@@ -544,8 +577,9 @@
     inputs = own_tokens.reshape(-1, width).astype(F32)
     normed_low = layer_norm(everyone.astype(F32), gain_one, shift_one).astype(BF16)
     bias_row = jnp.concatenate([packed_shift[:width], jnp.zeros((width,), F32), packed_shift[width:]])
-    bias_row = bias_row.reshape(3, share, blocks, PAIR)
-    half_bias = jnp.swapaxes(lax.dynamic_index_in_dim(bias_row, core, 1, keepdims=False), 0, 1).reshape(-1)
+    half_bias = jnp.concatenate(
+        [lax.dynamic_slice(bias_row, (part * width + core * columns,), (columns,)) for part in range(3)]
+    )
     packed = (jnp.dot(normed_low, half_packed, preferred_element_type=F32) + half_bias).astype(BF16)
     attended_heads, logsum = attend_forward(packed, low_blocks, begins)
 
@@ -591,16 +625,15 @@
         + [reduce_weight_grad.astype(BF16).reshape(devices, -1, width)],
         axis=1,
     )
-    grad_attended = against_rows(grad_proj, full_output).astype(BF16).reshape(2, local_rows, share, columns)
-    kept = lax.dynamic_index_in_dim(grad_attended, core, 2, keepdims=False)
-    came = lax.ppermute(
-        lax.dynamic_index_in_dim(grad_attended, 1 - core, 2, keepdims=False), "seq", swap_core
-    )
+    grad_attended = against_rows(grad_proj, full_output).astype(BF16)
+    take = lambda c: lax.dynamic_slice(grad_attended, (0, c * columns), (2 * local_rows, columns))
+    kept = take(core).reshape(2, local_rows, columns)
+    came = lax.ppermute(take(1 - core), "seq", swap_core).reshape(2, local_rows, columns)
     grad_heads, early = lax.optimization_barrier((interleave(kept, came), early))
     early_sum = scatter_sum(early.reshape(-1, width)).astype(F32)
     grad_packed = attend_backward(packed, attended_heads, grad_heads, logsum, high_blocks, begins)
     half_grad = outer_sum(normed_low, grad_packed).astype(BF16)
-    half_sums = jnp.sum(grad_packed.astype(F32), axis=0).reshape(blocks, 3, PAIR)
+    half_sums = jnp.sum(grad_packed.astype(F32), axis=0).reshape(3, columns)
     part_grad = against_rows(grad_packed, half_packed).astype(BF16)
     by_core = part_grad.reshape(2, share, local_rows, width)
     kept = lax.dynamic_index_in_dim(by_core, core, 1, keepdims=False)
@@ -617,36 +650,31 @@
         nothing = jnp.zeros_like(half)
         return [jnp.where(core == place_of, half, nothing) for place_of in range(share)]
 
-    packed_bias_grad = jnp.concatenate([block for part in (0, 2) for block in spread(half_sums[:, part].reshape(-1))])
+    packed_bias_grad = jnp.concatenate([block for part in (0, 2) for block in spread(half_sums[part])])
     small_grads = [gain_one_grad, shift_one_grad, packed_bias_grad, output_bias_grad, gain_two_grad, shift_two_grad, expand_bias_grad, reduce_bias_grad]
     if own_kernels:
-        chips = devices // share
-        small_rows = jnp.concatenate([g.reshape(chips, -1) for g in small_grads], axis=1)
-        small_rows = jnp.pad(small_rows, ((0, 0), (0, 1024 - share * small_count))).reshape(4, 2, 2, 8, 128)
+        small_rows = jnp.stack(
+            [jnp.pad(g.reshape(devices, -1), ((0, 0), (0, 128 - g.size // devices))) for g in small_grads], axis=1
+        ).reshape(4, 2, 2, share * 8, 128)
         own_half, other_half, small_sum = reduce_last(half_grad.reshape(4, 2, 2, share * rows, 3 * columns), small_rows)
         packed_halves = [jnp.where(core == c, own_half, other_half) for c in range(share)]
-        chip_sum, at, small_sum = small_sum.reshape(-1), 0, []
-        for size in sizes:
-            small_sum.append(lax.dynamic_slice(chip_sum, (at + core * size,), (size,)))
-            at += share * size
-        small_sum = jnp.concatenate(small_sum)
+        pieces = [small_sum[i, :size] for i, size in enumerate(sizes)]
     else:
         both_halves = scatter_sum(jnp.concatenate(spread(half_grad), axis=1)).astype(F32)
         packed_halves = [both_halves[:, c * 3 * columns : (c + 1) * 3 * columns] for c in range(share)]
         small_sum = scatter_sum(jnp.concatenate([g.reshape(devices, -1) for g in small_grads], axis=1))[0]
+        pieces, at = [], 0
+        for size in sizes:
+            pieces.append(small_sum[at : at + size])
+            at += size
     packed_sum = jnp.concatenate(
         [
-            packed_halves[c][:, (3 * g + part) * PAIR : (3 * g + part + 1) * PAIR]
+            packed_halves[c][:, part * columns : (part + 1) * columns]
             for part in range(3)
             for c in range(share)
-            for g in range(blocks)
         ],
         axis=1,
     )
-    pieces, at = [], 0
-    for size in sizes:
-        pieces.append(small_sum[at : at + size])
-        at += size
     expand_sum = jnp.concatenate(
         [early_sum[rows * (j + 1) : rows * (j + 2)] for j in range(pieces_per_row)], axis=1
     )

time: 477 us -> 418 us (0.88)
  Pallas kernels: 229 us -> 176 us
  local copies, waits for them, and re-layouts: 74.8 us -> 51.9 us
  waiting for transfers between devices: 14.7 us -> 33.2 us
    pallas_call x1, Pallas kernels: 70.4 us -> 26.5 us  [attend_forward(): pl.pallas_call(attend_kernel, name='attend_forward', out_shape=(jax.Shape...]
    all_gather x1, waiting for transfers between devices: 0.01 us -> 33.1 us  [gather_rows(): return lax.all_gather(shard, ('dp', 'seq'), axis=0, tiled=True)]
    ppermute x2 -> x1, waiting for transfers between devices: 14.7 us -> 0.01 us  [local(): lax.ppermute(take(1 - core), 'seq', swap_core)]
    pallas_call x1, Pallas kernels: 67.5 us -> 54.3 us  [attend_backward(): pl.pallas_call(attend_back_kernel, name='attend_backward', out_shape=jax....]
    dynamic_slice x4 -> x2, local copies, waits for them, and re-layouts: 9.27 us -> 0.18 us  [the longest x1 0.09 us: local(): lax.dynamic_slice(bias_row, (part * width + core * columns,), (columns,))]
    pallas_call x1, Pallas kernels: 40.7 us -> 48.9 us  [reduce_last(): pl.pallas_call(reduce_kernel, name='reduce_last', out_shape=(jax.ShapeDty...]
    unnamed x117 -> x83, local copies, waits for them, and re-layouts: 24.7 us -> 16.7 us
    concatenate x8 -> x2, local copies, waits for them, and re-layouts: 7.18 us -> 0.19 us  [the longest x1 0.19 us: local(): jnp.concatenate([jnp.pad(v.astype(F32), (0, 128 - v.shape[0])) for v in v...]
  transfers between devices with their start and end apart: 8 -> 7, of which waited for: 1 -> 1; matrix products, arithmetic and copies ran while one was open for 23% -> 21% of each run, Pallas kernels for 49% -> 32%
where the time goes in v2:
time: 418 us; the launch traced here: 411 us
  Pallas kernels  176 us (42%)
  matrix products  94 us (22%)
  local copies, waits for them, and re-layouts  51.9 us (12%)
  other arithmetic  35.2 us (8%)
  waiting for transfers between devices  33.2 us (8%)
  between operations  15.4 us (4%)
  starting transfers between devices  4.69 us (1%)
    pallas_call x1, Pallas kernels, attend_backward(): pl.pallas_call(attend_back_kernel, name='attend_backward', out_shape=jax....  54.3 us
    pallas_call x1, Pallas kernels, reduce_last(): pl.pallas_call(reduce_kernel, name='reduce_last', out_shape=(jax.ShapeDty...  48.9 us
    pallas_call x1, Pallas kernels, gather_first(): pl.pallas_call(gather_kernel, name='gather_first', out_shape=(jax.ShapeDt...  46.7 us
    dot_general x4, matrix products, against_rows(): lax.dot_general(first, second, (((1,), (1,)), ((), ())), preferred_elemen...  34.2 us
    all_gather x1, waiting for transfers between devices, gather_rows(): return lax.all_gather(shard, ('dp', 'seq'), axis=0, tiled=True)  33.1 us
    dot_general x4, matrix products, outer_sum(): lax.dot_general(first, second, (((0,), (0,)), ((), ())), preferred_elemen...  29 us
    pallas_call x1, Pallas kernels, attend_forward(): pl.pallas_call(attend_kernel, name='attend_forward', out_shape=(jax.Shape...  26.5 us
    unnamed x83, local copies, waits for them, and re-layouts  16.7 us
  transfers between devices with their start and end apart: 7, of which 1 were waited for; matrix products, arithmetic and copies ran while one was open for 21% of the time, Pallas kernels for 32%

profile of v2, /device:TPU:9, one launch (start us, length us, event | category | flops | bytes accessed | tf_op | source)
XLA Modules:
  0.0 410.7 jit_solution(10286620297106341193)
XLA Ops:
  19.4 46.7 %gather_first.1 = (bf16[2,2,512,768]{3,2,1,0:T(8,128)(2,1)}, bf16[2,512,768]{2,1,0:T(8,128)(2,1)}, bf16[4,2,2,2,24,1152]{5,4,3,2,1,0:T(8,128)(2,1)}, f32[4,2,2,2,8,128]{5,4,3,2,1,0:T(8,128)}) custom-call(bf16[2,512,768]{2,1,0:T(8,128)(2,1)} %token_ref.1, bf16[2,512,768]{2,1,0:T(8,128)(2,1)} %cotangent_ref.1, bf16[24,2304]{1,0:T(8,128)(2,1)} %weight_ref.1, ...), custom_call_target="tpu_custom_call" | custom-call | tf_op jit(solution)/shard_map/gather_first/pallas_call | solution.py:366
  66.7 1.2 copy.43
  70.3 2.4 convert_reduce_fusion.2
  73.8 1.5 add_convert_fusion.1
  75.4 5.9 %add_convert_fusion.packed_ref = bf16[2048,1152]{1,0:T(8,128)(2,1)} fusion(bf16[2048,768]{1,0:T(8,128)(2,1)S(1)} %bitcast.244, bf16[768,1152]{1,0:T(8,128)(2,1)S(1)} %bitcast.289, f32[1152]{0:T(1024)S(1)} %pad_maximum_fusion.9), kind=kOutput, calls=%fused_computation.12 | convolution fusion | flops 3628597248 | bytes 9638400 | tf_op jit(solution)/shard_map/dot_general | solution.py:583
  81.3 26.5 %attend_forward.1 = (bf16[2048,384]{1,0:T(8,128)(2,1)}, f32[6,2048]{1,0:T(8,128)}) custom-call(s32[2,8]{1,0:T(2,128)} %get-tuple-element.121.bounds_ref, bf16[2048,1152]{1,0:T(8,128)(2,1)} %add_convert_fusion.packed_ref, s32[1,2048]{1,0:T(1,128)} %bitcast.284), custom_call_target="tpu_custom_call" | custom-call | flops 3221225472 | bytes 7077888 | tf_op jit(solution)/shard_map/attend_forward/pallas_call | solution.py:122
  107.8 2.1 dynamic-slice_bitcast_fusion.3
  112.1 1.3 constant_dynamic-slice_fusion.3
  114.1 1.7 convert_reduce_fusion.4
  115.8 1.5 bitcast_select_fusion.5
  117.3 1.3 pad_maximum_fusion.1
  118.6 33.1 %all-gather.2.cloned.1.call-done = bf16[6912,768]{1,0:T(8,128)(2,1)} async-done(((bf16[216,768]{1,0:T(8,128)(2,1)}), bf16[6912,768]{1,0:T(8,128)(2,1)}) %all-gather.2.cloned.1.call-update) | async-done | bytes 10616848 | tf_op jit(solution)/shard_map/all_gather | solution.py:474
  151.7 2.6 slice.235
  154.4 4.8 %fusion.43 = (bf16[32,24,768]{2,1,0:T(8,128)(2,1)S(1)}, bf16[32,24,768]{2,1,0:T(8,128)(2,1)S(1)}, bf16[32,24,768]{2,1,0:T(8,128)(2,1)S(1)}, bf16[32,24,768]{2,1,0:T(8,128)(2,1)S(1)}, bf16[32,24,768]{2,1,0:T(8,128)(2,1)S(1)}) fusion(bf16[32,216,768]{2,1,0:T(8,128)(2,1)} %bitcast.234), kind=kLoop, calls=%fused_computation.187 | loop fusion | bytes 11796480 | tf_op jit(solution)/shard_map/slice | solution.py:554
  159.7 1.6 fusion.49
  161.9 9.8 %fusion.25 = f32[1024,3072]{1,0:T(8,128)} fusion(bf16[768,768]{1,0:T(8,128)(2,1)S(1)} %bitcast.262, bf16[768,768]{1,0:T(8,128)(2,1)S(1)} %bitcast.264, bf16[768,768]{1,0:T(8,128)(2,1)S(1)} %bitcast.266, bf16[768,768]{1,0:T(8,128)(2,1)S(1)} %bitcast.260, f32[1024,768]{1,0:T(8,128)S(1)} %get-tuple-element.117, f32[768]{0:T(1024)S(1)} %add.240, ...), kind=kOutput, calls=%fused_computation.70 | convolution fusion | flops 4854644736 | bytes 20461568 | tf_op jit(solution)/shard_map/dot_general | solution.py:599
  171.7 16.6 %convert_reduce_fusion = (f32[3072]{0:T(1024)S(1)}, bf16[1024,3072]{1,0:T(8,128)(2,1)}) fusion(f32[1024,3072]{1,0:T(8,128)} %fusion.25, f32[3072]{0:T(1024)S(1)} %add.243, bf16[1024,768]{1,0:T(8,128)(2,1)S(1)} %bitcast.253, bf16[3072,768]{1,0:T(8,128)(2,1)S(1)} %bitcast.241), kind=kOutput, calls=%fused_computation.9 | convolution fusion | flops 4904186880 | bytes 25190400 | tf_op jit(solution)/shard_map/dot_general | solution.py:26
  188.3 8.7 %multiply_reduce_fusion.1 = (f32[768]{0:T(1024)S(1)}, f32[1024]{0:T(1024)S(1)}, f32[768]{0:T(1024)S(1)}, f32[1024,768]{1,0:T(8,128)S(1)}) fusion(f32[1024,768]{1,0:T(8,128)S(1)} %get-tuple-element.117, f32[1024]{0:T(1024)S(1)} %fusion.31, f32[1024]{0:T(1024)S(1)} %broadcast_multiply_fusion.2, f32[768]{0:T(1024)S(1)} %mul.286, ...), kind=kOutput, calls=%fused_computation.52 | convolution fusion | flops 4857000960 | bytes 17323008 | tf_op jit(solution)/shard_map/dot_general | solution.py:26
  197.0 8.5 %convolution_convert_fusion.1 = bf16[768,3072]{1,0:T(8,128)(2,1)S(1)} fusion(bf16[1024,3072]{1,0:T(8,128)(2,1)} %get-tuple-element.120, f32[1024,768]{1,0:T(8,128)S(1)} %get-tuple-element.117, f32[768]{0:T(1024)S(1)} %add.240, f32[768]{0:T(1024)S(1)} %mul.286, f32[1024]{0:T(1024)S(1)} %fusion.31, f32[1024]{0:T(1024)S(1)} %broadcast_multiply_fusion.2), kind=kOutput, calls=%fused_computation.22 | convolution fusion | flops 4838129664 | bytes 14170112 | tf_op jit(solution)/shard_map/dot_general | solution.py:22
  205.6 1.6 fusion.42
  208.9 1.5 convolution_convert_fusion.5
  210.3 1.4 convolution_convert_fusion.4
  212.1 10.8 %convolution_convert_fusion = bf16[3072,768]{1,0:T(8,128)(2,1)S(1)} fusion(bf16[1024,768]{1,0:T(8,128)(2,1)S(1)} %get-tuple-element.76, f32[1024,3072]{1,0:T(8,128)} %fusion.25, f32[3072]{0:T(1024)S(1)} %add.243), kind=kOutput, calls=%fused_computation.21 | convolution fusion | flops 4865654784 | bytes 18886656 | tf_op jit(solution)/shard_map/dot_general | solution.py:22
  226.7 1.1 constant_dynamic-update-slice_fusion.8
  228.9 2.5 constant_dynamic-update-slice_fusion.6
  231.8 1.3 pad_maximum_fusion.3
  233.7 2.4 fusion.10
  236.4 13.5 %multiply_convert_fusion.4 = bf16[1024,768]{1,0:T(8,128)(2,1)S(1)} fusion(f32[1024,768]{1,0:T(8,128)} %copy-done.5, bf16[3072,768]{1,0:T(8,128)(2,1)} %bitcast.242, f32[1024]{0:T(1024)S(1)} %bitcast.274, f32[768]{0:T(1024)S(1)} %add.248, f32[1024,3072]{1,0:T(8,128)} %fusion.25, f32[3072]{0:T(1024)S(1)} %add.243), kind=kOutput, calls=%fused_computation.59 | convolution fusion | flops 4867227648 | bytes 22039552 | tf_op jit(solution)/shard_map/dot_general | solution.py:602
  252.0 1.2 collective-permute-start.1
  253.2 54.3 %attend_backward.1 = bf16[2048,1152]{1,0:T(8,128)(2,1)} custom-call(s32[2,8]{1,0:T(2,128)} %get-tuple-element.122.bounds_ref, bf16[2048,1152]{1,0:T(8,128)(2,1)} %add_convert_fusion.packed_ref, bf16[2048,384]{1,0:T(8,128)(2,1)} %get-tuple-element.31.o_ref, bf16[2048,384]{1,0:T(8,128)(2,1)} %bitcast.250, s32[1,2048]{1,0:T(1,128)} %bitcast.285, ...), custom_call_target="tpu_custom_call" | custom-call | flops 8053063680 | bytes 14155776 | tf_op jit(solution)/shard_map/attend_backward/pallas_call | solution.py:231
  307.5 7.5 %convolution_convert_fusion.2 = bf16[2048,768]{1,0:T(8,128)(2,1)S(1)} fusion(bf16[2048,1152]{1,0:T(8,128)(2,1)} %attend_backward.1, bf16[768,1152]{1,0:T(8,128)(2,1)} %bitcast.288), kind=kOutput, calls=%fused_computation.27 | convolution fusion | flops 3625451520 | bytes 9633792 | tf_op jit(solution)/shard_map/dot_general | solution.py:26
  315.1 1.4 dynamic-slice_bitcast_fusion
  318.1 1.6 fusion.28
  319.7 1.3 pad_maximum_fusion.2
  321.0 8.1 %convolution_convert_fusion.3 = bf16[768,1152]{1,0:T(8,128)(2,1)} fusion(bf16[2048,768]{1,0:T(8,128)(2,1)S(1)} %copy-done.10, bf16[2048,1152]{1,0:T(8,128)(2,1)} %attend_backward.1), kind=kOutput, calls=%fused_computation.28 | convolution fusion | flops 3624763392 | bytes 9633792 | tf_op jit(solution)/shard_map/dot_general | solution.py:22
  329.2 2.7 fusion.22
  332.0 1.6 copy-done.2
  333.6 1.6 fusion.21
  336.3 4.1 fusion.13
  341.6 1.6 collective-permute-start.4
  343.2 48.9 %reduce_last.1 = (f32[24,1152]{1,0:T(8,128)}, f32[24,1152]{1,0:T(8,128)}, f32[8,128]{1,0:T(8,128)}) custom-call(bf16[4,2,2,48,1152]{4,3,2,1,0:T(8,128)(2,1)} %bitcast.249, f32[4,2,2,16,128]{4,3,2,1,0:T(8,128)} %bitcast.269), custom_call_target="tpu_custom_call" | custom-call | tf_op jit(solution)/shard_map/reduce_last/pallas_call | solution.py:458
  392.0 1.2 slice_bitcast_fusion.5
  393.2 1.4 slice_bitcast_fusion
  395.7 1.2 slice_bitcast_fusion.1
  396.9 1.3 fusion.26
  398.2 1.3 pad_maximum_fusion.4
  399.5 1.5 fusion.45
  401.7 1.6 slice.254
  (176 shorter events, 35.7 us)
Async XLA Ops:
  7.2 59.1 %copy-start.22 = (s32[2,1,4]{2,1,0:T(1,128)S(1)}, s32[2,1,4]{2,1,0:T(1,128)}, u32[]{:S(2)}) copy-start(s32[2,1,4]{2,1,0:T(1,128)} %param.17) | copy-start | bytes 100
  7.2 144.5 %all-gather.2.cloned.1.call-start = ((), (), s32[]{:S(2)}) async-start(), calls=%async_computation.1 | async-start | bytes 10948608 | tf_op jit(solution)/shard_map/all_gather | solution.py:474
  19.4 46.7 %copy-start.19 = (bf16[216,768]{1,0:T(8,128)(2,1)}, bf16[216,768]{1,0:T(8,128)(2,1)S(1)}, u32[]{:S(2)}) copy-start(bf16[216,768]{1,0:T(8,128)(2,1)S(1)} %constant_dynamic-update-slice_fusion) | copy-start | bytes 995332
  66.1 6.6 %copy-start = (bf16[2,2,512,768]{3,2,1,0:T(8,128)(2,1)S(1)}, bf16[2,2,512,768]{3,2,1,0:T(8,128)(2,1)}, u32[]{:S(2)}) copy-start(bf16[2,2,512,768]{3,2,1,0:T(8,128)(2,1)} %get-tuple-element.27) | copy-start | bytes 9437188
  66.2 333.4 %reduce-scatter.2.cloned.1.call-start = ((), (), s32[]{:S(2)}) async-start(), calls=%async_computation.2 | async-start | bytes 10948608 | tf_op jit(solution)/shard_map/reduce_scatter | solution.py:478
  66.6 7.2 %copy-start.20 = (s32[2048]{0:T(1024)}, s32[2048]{0:T(1024)S(1)}, u32[]{:S(2)}) copy-start(s32[2048]{0:T(1024)S(1)} %get-tuple-element.51) | copy-start | bytes 24580
  73.8 1.5 copy-start.23
  109.9 5.9 %collective-permute-start = (bf16[2,512,384]{2,1,0:T(8,128)(2,1)}, bf16[2,512,384]{2,1,0:T(8,128)(2,1)}, u32[]{:S(2)}, u32[]{:S(2)}) collective-permute-start(bf16[2,512,384]{2,1,0:T(8,128)(2,1)} %dynamic-slice_bitcast_fusion.3), channel_id=1, source_target_pairs={{0,1},{1,0},{2,3},{3,2},{4,5},{5,4},{6,7},{7,6},{8,9},{9,8},{10,11... | collective-permute-start | bytes 2359304 | tf_op jit(solution)/shard_map/ppermute | solution.py:588
  112.1 2.0 copy-start.3
  112.1 3.7 copy-start.15
  154.3 17.3 %copy-start.8 = (bf16[32,96,768]{2,1,0:T(8,128)(2,1)}, bf16[32,96,768]{2,1,0:T(8,128)(2,1)S(1)}, u32[]{:S(2)}) copy-start(bf16[32,96,768]{2,1,0:T(8,128)(2,1)S(1)} %slice.235) | copy-start | bytes 14155780
  154.4 4.9 %copy-start.13 = (bf16[2,512,768]{2,1,0:T(8,128)(2,1)S(1)}, bf16[2,512,768]{2,1,0:T(8,128)(2,1)}, u32[]{:S(2)}) copy-start(bf16[2,512,768]{2,1,0:T(8,128)(2,1)} %pad_maximum_fusion.1) | copy-start | bytes 4718596
  154.4 5.3 %copy-start.17 = (bf16[2,1,512,768]{3,2,1,0:T(8,128)(2,1)S(1)}, bf16[2,1,512,768]{3,2,1,0:T(8,128)(2,1)}, u32[]{:S(2)}) copy-start(bf16[2,1,512,768]{3,2,1,0:T(8,128)(2,1)} %constant_dynamic-slice_fusion.3) | copy-start | bytes 4718596
  159.2 2.7 copy-start.18
  161.3 44.2 %copy-start.5 = (f32[1024,768]{1,0:T(8,128)}, f32[1024,768]{1,0:T(8,128)S(1)}, u32[]{:S(2)}) copy-start(f32[1024,768]{1,0:T(8,128)S(1)} %get-tuple-element.117) | copy-start | bytes 9437188
  161.9 9.8 %copy-start.14 = (bf16[2,512,768]{2,1,0:T(8,128)(2,1)S(1)}, bf16[2,512,768]{2,1,0:T(8,128)(2,1)}, u32[]{:S(2)}) copy-start(bf16[2,512,768]{2,1,0:T(8,128)(2,1)} %get-tuple-element.53) | copy-start | bytes 4718596
  205.5 1.7 copy-start.4
  207.2 1.7 copy-start.1
  223.0 8.4 %collective-permute-start.2 = (bf16[1024,384]{1,0:T(8,128)(2,1)S(1)}, bf16[1024,384]{1,0:T(8,128)(2,1)S(1)}, u32[]{:S(2)}, u32[]{:S(2)}) collective-permute-start(bf16[1024,384]{1,0:T(8,128)(2,1)S(1)} %constant_dynamic-slice_fusion), channel_id=1, source_target_pairs={{0,1},{1,0},{2,3},{3,2},{4,5},{5,4},{6,7},{7,6},{8,9},{9,8},{10,11... | collective-permute-start | bytes 2359304 | tf_op jit(solution)/shard_map/ppermute | solution.py:631
  249.9 1.1 copy-start.16
  252.0 66.1 %collective-permute-start.1 = (bf16[512,768]{1,0:T(8,128)(2,1)}, bf16[512,768]{1,0:T(8,128)(2,1)}, u32[]{:S(2)}, u32[]{:S(2)}) collective-permute-start(bf16[512,768]{1,0:T(8,128)(2,1)} %dynamic-slice_bitcast_fusion.2), channel_id=1, source_target_pairs={{0,2},{1,3},{2,0},{3,1},{4,6},{5,7},{6,4},{7,5},{8,10},{9,11},{10,... | collective-permute-start | bytes 2359304 | tf_op jit(solution)/shard_map/ppermute | solution.py:519
  307.5 9.5 %copy-start.9 = (bf16[2048,1152]{1,0:T(8,128)(2,1)S(1)}, bf16[2048,1152]{1,0:T(8,128)(2,1)}, u32[]{:S(2)}) copy-start(bf16[2048,1152]{1,0:T(8,128)(2,1)} %attend_backward.1) | copy-start | bytes 14155780
  315.0 2.7 copy-start.11
  316.4 12.7 %collective-permute-start.3 = (bf16[2,512,768]{2,1,0:T(8,128)(2,1)}, bf16[2,512,768]{2,1,0:T(8,128)(2,1)}, u32[]{:S(2)}, u32[]{:S(2)}) collective-permute-start(bf16[2,512,768]{2,1,0:T(8,128)(2,1)} %dynamic-slice_bitcast_fusion), channel_id=1, source_target_pairs={{0,1},{1,0},{2,3},{3,2},{4,5},{5,4},{6,7},{7,6},{8,9},{9,8},{10,11... | collective-permute-start | bytes 4718600 | tf_op jit(solution)/shard_map/ppermute | solution.py:640
  318.1 2.9 copy-start.10
  321.0 8.1 %copy-start.12 = (bf16[2048,768]{1,0:T(8,128)(2,1)S(1)}, bf16[2048,768]{1,0:T(8,128)(2,1)}, u32[]{:S(2)}) copy-start(bf16[2048,768]{1,0:T(8,128)(2,1)} %copy-done.11) | copy-start | bytes 9437188
  331.9 1.7 copy-start.2
  340.4 1.1 copy-start.6
  341.6 55.3 %copy-start.7 = (bf16[1024,768]{1,0:T(8,128)(2,1)S(1)}, bf16[1024,768]{1,0:T(8,128)(2,1)}, u32[]{:S(2)}) copy-start(bf16[1024,768]{1,0:T(8,128)(2,1)} %copy-done.6) | copy-start | bytes 4718596
  341.6 55.3 %collective-permute-start.4 = (bf16[512,768]{1,0:T(8,128)(2,1)S(1)}, bf16[512,768]{1,0:T(8,128)(2,1)}, u32[]{:S(2)}, u32[]{:S(2)}) collective-permute-start(bf16[512,768]{1,0:T(8,128)(2,1)S(1)} %dynamic-slice_bitcast_fusion.1), channel_id=1, source_target_pairs={{0,2},{1,3},{2,0},{3,1},{4,6},{5,7},{6,4},{7,5},{8,10},{9,11},{10,... | collective-permute-start | bytes 2359304 | tf_op jit(solution)/shard_map/ppermute | solution.py:519
  396.9 2.6 copy-start.21
Sparse Core Ops, SparseCore 0:
  66.3 85.3 all-gather.1
  233.3 142.9 reduce-scatter.1

commit v3 on v2

--- a/solution.py
+++ b/solution.py
@@ -156,7 +156,7 @@
     blocks = packed_ref.shape[0] // TILE
     groups = o_ref.shape[1] // PAIR
     half = lax.broadcasted_iota(jnp.int32, (8, PAIR), 1) // HD
-    picks = (half == lax.broadcasted_iota(jnp.int32, (8, PAIR), 0)).astype(F32)
+    picks = (half == lax.broadcasted_iota(jnp.int32, (8, PAIR), 0)).astype(F32).astype(BF16)
     for g in range(groups):
         column = slice(g * PAIR, (g + 1) * PAIR)
         for block in range(blocks):
@@ -164,13 +164,9 @@
             key_t[column, at] = packed_ref[at, third(packed_ref, 1, g)].T
             query_t[column, at] = jnp.zeros((PAIR, TILE), F32)
             product = o_ref[at, column].astype(F32) * go_ref[at, column].astype(F32)
-            delta[g * 8 : (g + 1) * 8, at] = lax.dot_general(
-                picks,
-                product,
-                (((1,), (1,)), ((), ())),
-                precision=lax.Precision.HIGHEST,
-                preferred_element_type=F32,
-            )
+            coarse = product.astype(BF16)
+            fine = (product - coarse.astype(F32)).astype(BF16)
+            delta[g * 8 : (g + 1) * 8, at] = against_rows(picks, coarse) + against_rows(picks, fine)
 
     def one_key_block(j, carry):
         there = pl.ds(pl.multiple_of(j * TILE, TILE), TILE)
@@ -290,9 +286,13 @@
 
 
 def gather_kernel(
-    token_ref, cotangent_ref, weight_ref, tiny_ref, all_tokens, all_cotangent, all_half, all_tiny, local_sem, *semaphores
+    token_ref, weight_ref, *rest
 ):
+    vector_refs, (all_tokens, all_half, all_tiny, tiny_ref, local_sem), semaphores = rest[:8], rest[8:13], rest[13:]
     z, x, y, core = position()
+    tiny_ref[...] = jnp.zeros_like(tiny_ref)
+    for i, vector_ref in enumerate(vector_refs):
+        tiny_ref[i, : vector_ref.shape[0]] = vector_ref[...].astype(F32)
     token_sems, half_sems, tiny_sems = [semaphores[2 * i : 2 * i + 2] for i in range(3)]
     meet(z, x, y, core)
     core_twin, y_twin, x_twin = device(z, x, y, 1 - core), device(z, x, 1 - y, core), device(z, 1 - x, y, core)
@@ -306,17 +306,16 @@
     sent = []
     local = [
         pltpu.make_async_copy(token_ref.at[y], all_tokens.at[y, core], local_sem.at[0]),
-        pltpu.make_async_copy(cotangent_ref.at[y], all_cotangent.at[y], local_sem.at[1]),
-        pltpu.make_async_copy(tiny_ref, all_tiny.at[z, x, y, core], local_sem.at[2]),
+        pltpu.make_async_copy(tiny_ref, all_tiny.at[z, x, y, core], local_sem.at[1]),
     ]
     swaps = [send(tiny_ref, all_tiny.at[z, x, y, core], tiny_sems, 0, core_twin)]
     for part in range(3):
         mine = all_half.at[z, x, y, core, :, part * columns : (part + 1) * columns]
-        local.append(pltpu.make_async_copy(weight_part(part, core), mine, local_sem.at[3 + part]))
+        local.append(pltpu.make_async_copy(weight_part(part, core), mine, local_sem.at[2 + part]))
         swaps.append(send(weight_part(part, 1 - core), mine, half_sems, (0, 16, 17)[part], core_twin))
-    for copy in local[2:] + local[:2]:
+    for copy in local[1:] + local[:1]:
         copy.start()
-    for copy in local[2:]:
+    for copy in local[1:]:
         copy.wait()
     for copy in swaps:
         copy.wait_recv()
@@ -324,7 +323,6 @@
     own = [(whole.at[z, x, y], sems) for whole, sems in streams]
     over_y = [send(piece, piece, sems, 1, y_twin) for piece, sems in own]
     token_y = send(token_ref.at[1 - y], all_tokens.at[y, core], token_sems, 0, y_twin)
-    cotangent_y = send(cotangent_ref.at[1 - y], all_cotangent.at[y], token_sems, 3, y_twin)
     token_own = send(token_ref.at[y], all_tokens.at[y, core], token_sems, 1, core_twin)
     along_z, over_x = {}, []
 
@@ -349,15 +347,14 @@
                 along_z[p, t, i].wait_recv()
                 piece = whole.at[source, x, row]
                 over_x.append(send(piece, piece, sems, 8 + 4 * p + t, x_twin))
-    for copy in over_x + [token_own, token_next, cotangent_y]:
+    for copy in over_x + [token_own, token_next]:
         copy.wait_recv()
-    for copy in sent + over_y + [token_y, token_own, token_next, cotangent_y] + list(along_z.values()) + over_x:
+    for copy in sent + over_y + [token_y, token_own, token_next] + list(along_z.values()) + over_x:
         copy.wait_send()
     local[0].wait()
-    local[1].wait()
-
-
-def gather_first(tokens, cotangent, weight, tiny):
+
+
+def gather_first(tokens, weight, vectors):
     _, local_rows, width = tokens.shape
     rows, columns = weight.shape
     anywhere = pl.BlockSpec(memory_space=pl.ANY)
@@ -368,15 +365,14 @@
         name="gather_first",
         out_shape=(
             jax.ShapeDtypeStruct((2, 2, local_rows, width), BF16),
-            jax.ShapeDtypeStruct((2, local_rows, width), BF16),
             jax.ShapeDtypeStruct((4, 2, 2, 2, rows, columns // 2), BF16),
             jax.ShapeDtypeStruct((4, 2, 2, 2, 8, 128), F32),
         ),
-        in_specs=[near] * 4,
-        out_specs=[anywhere] * 4,
-        scratch_shapes=[sems((6,)), sems((4,)), sems((4,)), sems((18,)), sems((18,)), sems((16,)), sems((16,))],
+        in_specs=[near] * (2 + len(vectors)),
+        out_specs=[anywhere] * 3,
+        scratch_shapes=[pltpu.VMEM((8, 128), F32), sems((5,)), sems((3,)), sems((3,)), sems((18,)), sems((18,)), sems((16,)), sems((16,))],
         compiler_params=pltpu.CompilerParams(collective_id=1, has_side_effects=True),
-    )(tokens, cotangent, weight, tiny)
+    )(tokens, weight, *vectors)
 
 
 def reduce_kernel(big_ref, tiny_ref, own_ref, other_ref, sum_ref, *scratch):
@@ -507,11 +503,15 @@
     swap_micro = [(s, (s + share) % groups) for s in range(groups)]
     swap_core = [(s, s ^ 1) for s in range(groups)]
 
+    def swap_of(both):
+        return lax.dynamic_index_in_dim(both, 1 - mine, 0, keepdims=False)
+
+    def placed(both, came):
+        kept = lax.dynamic_index_in_dim(both, mine, 0, keepdims=False)
+        return jnp.stack([jnp.where(mine == 0, kept, came), jnp.where(mine == 0, came, kept)])
+
     def own_micro(both):
-        kept = lax.dynamic_index_in_dim(both, mine, 0, keepdims=False)
-        sent = lax.dynamic_index_in_dim(both, 1 - mine, 0, keepdims=False)
-        came = lax.ppermute(sent, "seq", swap_micro)
-        return jnp.stack([jnp.where(mine == 0, kept, came), jnp.where(mine == 0, came, kept)])
+        return placed(both, lax.ppermute(swap_of(both), "seq", swap_micro))
 
     def home_micro(blocks):
         kept = lax.dynamic_index_in_dim(blocks, mine, 0, keepdims=False)
@@ -529,25 +529,24 @@
     small_count = sum(sizes)
     pieces_per_row = hidden_width // width
     rows = output_weight.shape[0]
-    tiny = jnp.concatenate([jnp.pad(v.astype(F32), (0, 128 - v.shape[0])) for v in vectors]).reshape(8, 128)
     own_kernels = devices == 32 and groups == 4
     if own_kernels:
-        all_tokens, own_cotangent, half_packed, all_tiny = gather_first(tokens, cotangent, packed_weight, tiny)
+        all_tokens, half_packed, all_tiny = gather_first(tokens, packed_weight, vectors)
         everyone = all_tokens.reshape(bucket, width)
         own_tokens = lax.dynamic_index_in_dim(all_tokens, core, 1, keepdims=False)
         half_packed = half_packed.reshape(width, 3 * columns)
     else:
-        own_tokens, own_cotangent = own_micro(tokens), own_micro(cotangent)
+        own_tokens = own_micro(tokens)
         everyone = interleave(own_tokens, lax.ppermute(own_tokens, "seq", swap_core))
         full_packed = gather_rows(packed_weight)
         half_packed = jnp.concatenate(
             [lax.dynamic_slice(full_packed, (0, part * width + core * columns), (width, columns)) for part in range(3)], axis=1
         )
+        tiny = jnp.concatenate([jnp.pad(v.astype(F32), (0, 128 - v.shape[0])) for v in vectors]).reshape(8, 128)
         all_tiny = gather_rows(tiny)
     small_all = all_tiny.reshape(devices, 8, 128)
     expand_blocks = [expand_weight[:, j * width : (j + 1) * width] for j in range(pieces_per_row)]
     second_shard = jnp.concatenate([output_weight] + expand_blocks + [reduce_weight])
-    small_all, second_shard = lax.optimization_barrier((small_all, second_shard))
     second = gather_rows(second_shard).reshape(devices, -1, width)
     full_output = second[:, :rows].reshape(width, width)
     full_expand = jnp.concatenate(
@@ -581,7 +580,12 @@
         [lax.dynamic_slice(bias_row, (part * width + core * columns,), (columns,)) for part in range(3)]
     )
     packed = (jnp.dot(normed_low, half_packed, preferred_element_type=F32) + half_bias).astype(BF16)
+    packed, cotangent_sent = lax.optimization_barrier((packed, swap_of(cotangent)))
     attended_heads, logsum = attend_forward(packed, low_blocks, begins)
+    attended_heads, cotangent_came = lax.optimization_barrier(
+        (attended_heads, lax.ppermute(cotangent_sent, "seq", swap_micro))
+    )
+    own_cotangent = placed(cotangent, cotangent_came)
 
     by_core = attended_heads.reshape(2, share, local_rows, columns)
     kept = lax.dynamic_index_in_dim(by_core, core, 1, keepdims=False)

time: 418 us -> 398 us (0.952)
  waiting for transfers between devices: 33.2 us -> 8.46 us
  Pallas kernels: 176 us -> 185 us
  local copies, waits for them, and re-layouts: 51.9 us -> 47.7 us
    all_gather x1, waiting for transfers between devices: 33.1 us -> 2.54 us  [gather_rows(): return lax.all_gather(shard, ('dp', 'seq'), axis=0, tiled=True)]
    pallas_call x1, Pallas kernels: 46.7 us -> 55.3 us  [gather_first(): pl.pallas_call(gather_kernel, name='gather_first', out_shape=(jax.ShapeDt...]
    ppermute x0 -> x1, waiting for transfers between devices: none -> 5.86 us  [local(): lax.ppermute(cotangent_sent, 'seq', swap_micro)]
    pad x8 -> x0, local copies, waits for them, and re-layouts: 5.28 us -> none  [local(): jnp.pad(v.astype(F32), (0, 128 - v.shape[0]))]
    unnamed x83 -> x82, local copies, waits for them, and re-layouts: 16.7 us -> 15.7 us
  transfers between devices with their start and end apart: 7 -> 8, of which waited for: 1 -> 2; matrix products, arithmetic and copies ran while one was open for 21% -> 23% of each run, Pallas kernels for 32% -> 48%
where the time goes in v3:
time: 398 us; the launch traced here: 390 us
  Pallas kernels  185 us (46%)
  matrix products  93.8 us (24%)
  local copies, waits for them, and re-layouts  47.7 us (12%)
  other arithmetic  36.3 us (9%)
  between operations  15.4 us (4%)
  waiting for transfers between devices  8.46 us (2%)
    pallas_call x1, Pallas kernels, gather_first(): pl.pallas_call(gather_kernel, name='gather_first', out_shape=(jax.ShapeDt...  55.3 us
    pallas_call x1, Pallas kernels, attend_backward(): pl.pallas_call(attend_back_kernel, name='attend_backward', out_shape=jax....  54.4 us
    pallas_call x1, Pallas kernels, reduce_last(): pl.pallas_call(reduce_kernel, name='reduce_last', out_shape=(jax.ShapeDty...  48.2 us
    dot_general x4, matrix products, against_rows(): lax.dot_general(first, second, (((1,), (1,)), ((), ())), preferred_elemen...  34.1 us
    dot_general x4, matrix products, outer_sum(): lax.dot_general(first, second, (((0,), (0,)), ((), ())), preferred_elemen...  29.3 us
    pallas_call x1, Pallas kernels, attend_forward(): pl.pallas_call(attend_kernel, name='attend_forward', out_shape=(jax.Shape...  27.5 us
    unnamed x82, local copies, waits for them, and re-layouts  15.7 us
    dot_general x1, matrix products, local(): jnp.dot(active_low, full_reduce, preferred_element_type=F32) + reduce_shift  13.1 us
  transfers between devices with their start and end apart: 8, of which 2 were waited for; matrix products, arithmetic and copies ran while one was open for 23% of the time, Pallas kernels for 48%

profile of v3, /device:TPU:9, one launch (start us, length us, event | category | flops | bytes accessed | tf_op | source)
XLA Modules:
  0.0 389.8 jit_solution(9403138963244775427)
XLA Ops:
  12.8 55.3 %gather_first.1 = (bf16[2,2,512,768]{3,2,1,0:T(8,128)(2,1)}, bf16[4,2,2,2,24,1152]{5,4,3,2,1,0:T(8,128)(2,1)}, f32[4,2,2,2,8,128]{5,4,3,2,1,0:T(8,128)}) custom-call(bf16[2,512,768]{2,1,0:T(8,128)(2,1)} %token_ref.1, bf16[24,2304]{1,0:T(8,128)(2,1)} %weight_ref.1, bf16[24]{0:T(256)(128)(2,1)} %rest_0_.1, bf16[24]{0:T(256)(128)(2,1)} %rest_1_.1, ...), custom_call_target="tpu_custom_call" | custom-call | tf_op jit(solution)/shard_map/gather_first/pallas_call | solution.py:363
  69.3 1.4 fusion.48
  71.1 2.1 dynamic-slice_bitcast_fusion.4
  73.2 2.4 convert_reduce_fusion.2
  76.7 1.3 add_convert_fusion.1
  78.2 5.9 %add_convert_fusion.packed_ref = bf16[2048,1152]{1,0:T(8,128)(2,1)} fusion(bf16[2048,768]{1,0:T(8,128)(2,1)S(1)} %bitcast.260, bf16[768,1152]{1,0:T(8,128)(2,1)S(1)} %bitcast.311, f32[1152]{0:T(1024)S(1)} %pad_maximum_fusion.10), kind=kOutput, calls=%fused_computation.12 | convolution fusion | flops 3628597248 | bytes 9638400 | tf_op jit(solution)/shard_map/dot_general | solution.py:582
  85.6 27.5 %attend_forward.1 = (bf16[2048,384]{1,0:T(8,128)(2,1)}, f32[6,2048]{1,0:T(8,128)}) custom-call(s32[2,8]{1,0:T(2,128)} %get-tuple-element.125.bounds_ref, bf16[2048,1152]{1,0:T(8,128)(2,1)} %add_convert_fusion.packed_ref, s32[1,2048]{1,0:T(1,128)} %bitcast.306), custom_call_target="tpu_custom_call" | custom-call | flops 3221225472 | bytes 7077888 | tf_op jit(solution)/shard_map/attend_forward/pallas_call | solution.py:122
  113.1 5.9 %collective-permute-done = bf16[512,768]{1,0:T(8,128)(2,1)} collective-permute-done((bf16[512,768]{1,0:T(8,128)(2,1)}, bf16[512,768]{1,0:T(8,128)(2,1)}, u32[]{:S(2)}, u32[]{:S(2)}) %collective-permute-start) | collective-permute-done | bytes 786464 | tf_op jit(solution)/shard_map/ppermute | solution.py:586
  118.9 2.1 dynamic-slice_bitcast_fusion.3
  121.0 1.2 collective-permute-start.1
  123.5 1.3 constant_dynamic-slice_fusion.3
  125.5 1.5 fusion.28
  127.0 1.7 convert_reduce_fusion.4
  128.7 1.3 bitcast_select_fusion.7
  130.0 1.3 pad_maximum_fusion.1
  131.3 2.5 all-gather.2.cloned.1.call-done
  133.8 2.6 slice.238
  136.5 4.8 %fusion.45 = (bf16[32,24,768]{2,1,0:T(8,128)(2,1)S(1)}, bf16[32,24,768]{2,1,0:T(8,128)(2,1)S(1)}, bf16[32,24,768]{2,1,0:T(8,128)(2,1)S(1)}, bf16[32,24,768]{2,1,0:T(8,128)(2,1)S(1)}, bf16[32,24,768]{2,1,0:T(8,128)(2,1)S(1)}) fusion(bf16[32,216,768]{2,1,0:T(8,128)(2,1)} %bitcast.250), kind=kLoop, calls=%fused_computation.192 | loop fusion | bytes 11796480 | tf_op jit(solution)/shard_map/slice | solution.py:553
  141.8 1.6 fusion.51
  144.0 9.8 %fusion.25 = f32[1024,3072]{1,0:T(8,128)} fusion(bf16[768,768]{1,0:T(8,128)(2,1)S(1)} %bitcast.278, bf16[768,768]{1,0:T(8,128)(2,1)S(1)} %bitcast.280, bf16[768,768]{1,0:T(8,128)(2,1)S(1)} %bitcast.282, bf16[768,768]{1,0:T(8,128)(2,1)S(1)} %bitcast.276, f32[1024,768]{1,0:T(8,128)S(1)} %get-tuple-element.121, f32[768]{0:T(1024)S(1)} %add.227, ...), kind=kOutput, calls=%fused_computation.71 | convolution fusion | flops 4854644736 | bytes 20461568 | tf_op jit(solution)/shard_map/dot_general | solution.py:603
  153.8 16.6 %convert_reduce_fusion = (f32[3072]{0:T(1024)S(1)}, bf16[1024,3072]{1,0:T(8,128)(2,1)}) fusion(f32[1024,3072]{1,0:T(8,128)} %fusion.25, f32[3072]{0:T(1024)S(1)} %add.230, bf16[1024,768]{1,0:T(8,128)(2,1)S(1)} %bitcast.269, bf16[3072,768]{1,0:T(8,128)(2,1)S(1)} %bitcast.257), kind=kOutput, calls=%fused_computation.9 | convolution fusion | flops 4904186880 | bytes 25190400 | tf_op jit(solution)/shard_map/dot_general | solution.py:26
  170.4 8.7 %multiply_reduce_fusion.1 = (f32[768]{0:T(1024)S(1)}, f32[1024]{0:T(1024)S(1)}, f32[768]{0:T(1024)S(1)}, f32[1024,768]{1,0:T(8,128)S(1)}) fusion(f32[1024,768]{1,0:T(8,128)S(1)} %get-tuple-element.121, f32[1024]{0:T(1024)S(1)} %fusion.33, f32[1024]{0:T(1024)S(1)} %broadcast_multiply_fusion.2, f32[768]{0:T(1024)S(1)} %mul.298, ...), kind=kOutput, calls=%fused_computation.52 | convolution fusion | flops 4857000960 | bytes 17323008 | tf_op jit(solution)/shard_map/dot_general | solution.py:26
  179.1 8.5 %convolution_convert_fusion.1 = bf16[768,3072]{1,0:T(8,128)(2,1)S(1)} fusion(bf16[1024,3072]{1,0:T(8,128)(2,1)} %get-tuple-element.124, f32[1024,768]{1,0:T(8,128)S(1)} %get-tuple-element.121, f32[768]{0:T(1024)S(1)} %add.227, f32[768]{0:T(1024)S(1)} %mul.298, f32[1024]{0:T(1024)S(1)} %fusion.33, f32[1024]{0:T(1024)S(1)} %broadcast_multiply_fusion.2), kind=kOutput, calls=%fused_computation.22 | convolution fusion | flops 4838129664 | bytes 14170112 | tf_op jit(solution)/shard_map/dot_general | solution.py:22
  187.7 1.5 fusion.44
  189.2 1.5 convert_reduce_fusion.5
  190.9 1.5 convolution_convert_fusion.5
  192.3 1.4 convolution_convert_fusion.4
  194.1 11.0 %convolution_convert_fusion = bf16[3072,768]{1,0:T(8,128)(2,1)S(1)} fusion(bf16[1024,768]{1,0:T(8,128)(2,1)S(1)} %get-tuple-element.80, f32[1024,3072]{1,0:T(8,128)} %fusion.25, f32[3072]{0:T(1024)S(1)} %add.230), kind=kOutput, calls=%fused_computation.21 | convolution fusion | flops 4865654784 | bytes 18886656 | tf_op jit(solution)/shard_map/dot_general | solution.py:22
  211.1 2.5 constant_dynamic-update-slice_fusion.6
  213.9 1.3 pad_maximum_fusion.4
  215.7 2.4 fusion.10
  218.5 13.1 %multiply_convert_fusion.4 = bf16[1024,768]{1,0:T(8,128)(2,1)S(1)} fusion(f32[1024,768]{1,0:T(8,128)} %copy-done.7, bf16[3072,768]{1,0:T(8,128)(2,1)} %bitcast.258, f32[1024]{0:T(1024)S(1)} %bitcast.290, f32[768]{0:T(1024)S(1)} %add.235, f32[1024,3072]{1,0:T(8,128)} %fusion.25, f32[3072]{0:T(1024)S(1)} %add.230), kind=kOutput, calls=%fused_computation.59 | convolution fusion | flops 4867227648 | bytes 22039552 | tf_op jit(solution)/shard_map/dot_general | solution.py:606
  234.3 54.4 %attend_backward.1 = bf16[2048,1152]{1,0:T(8,128)(2,1)} custom-call(s32[2,8]{1,0:T(2,128)} %get-tuple-element.126.bounds_ref, bf16[2048,1152]{1,0:T(8,128)(2,1)} %add_convert_fusion.packed_ref, bf16[2048,384]{1,0:T(8,128)(2,1)} %get-tuple-element.34.o_ref, bf16[2048,384]{1,0:T(8,128)(2,1)} %bitcast.266, s32[1,2048]{1,0:T(1,128)} %bitcast.307, ...), custom_call_target="tpu_custom_call" | custom-call | flops 8053063680 | bytes 14155776 | tf_op jit(solution)/shard_map/attend_backward/pallas_call | solution.py:227
  288.6 7.4 %convolution_convert_fusion.2 = bf16[2048,768]{1,0:T(8,128)(2,1)S(1)} fusion(bf16[2048,1152]{1,0:T(8,128)(2,1)} %attend_backward.1, bf16[768,1152]{1,0:T(8,128)(2,1)} %bitcast.310), kind=kOutput, calls=%fused_computation.27 | convolution fusion | flops 3625451520 | bytes 9633792 | tf_op jit(solution)/shard_map/dot_general | solution.py:26
  296.0 1.3 dynamic-slice_bitcast_fusion
  299.0 1.6 fusion.30
  300.6 1.3 pad_maximum_fusion.2
  301.9 8.3 %convolution_convert_fusion.3 = bf16[768,1152]{1,0:T(8,128)(2,1)} fusion(bf16[2048,768]{1,0:T(8,128)(2,1)S(1)} %copy-done.12, bf16[2048,1152]{1,0:T(8,128)(2,1)} %attend_backward.1), kind=kOutput, calls=%fused_computation.28 | convolution fusion | flops 3624763392 | bytes 9633792 | tf_op jit(solution)/shard_map/dot_general | solution.py:22
  310.2 2.7 fusion.22
  313.0 1.6 copy-done.2
  314.6 1.6 fusion.21
  317.3 4.3 %fusion.13 = bf16[1024,768]{1,0:T(8,128)(2,1)S(1)} fusion(f32[2,512,768]{2,1,0:T(8,128)} %copy-done.2, f32[1024,768]{1,0:T(8,128)} %copy-done.1, f32[1024]{0:T(1024)S(1)} %bitcast.303, f32[1024]{0:T(1024)S(1)} %get-tuple-element.112, f32[1024]{0:T(1024)S(1)} %bitcast.301, f32[1024]{0:T(1024)S(1)} %get-tuple-element.111, f32[768]{0:T(1024)S(1)} %mul.290, ...), kind=kLoop, calls=%fused_computation.31 | loop fusion | flops 11796480 | bytes 11037700 | tf_op jit(solution)/shard_map/convert_element_type | solution.py:648
  322.9 48.2 %reduce_last.1 = (f32[24,1152]{1,0:T(8,128)}, f32[24,1152]{1,0:T(8,128)}, f32[8,128]{1,0:T(8,128)}) custom-call(bf16[4,2,2,48,1152]{4,3,2,1,0:T(8,128)(2,1)} %bitcast.265, f32[4,2,2,16,128]{4,3,2,1,0:T(8,128)} %bitcast.285), custom_call_target="tpu_custom_call" | custom-call | tf_op jit(solution)/shard_map/reduce_last/pallas_call | solution.py:454
  372.3 1.4 slice_bitcast_fusion
  376.0 1.3 fusion.26
  377.3 1.3 pad_maximum_fusion.5
  378.6 1.5 fusion.47
  380.8 1.6 slice.257
  (167 shorter events, 30.9 us)
Async XLA Ops:
  7.2 126.6 %all-gather.2.cloned.1.call-start = ((), (), s32[]{:S(2)}) async-start(), calls=%async_computation.1 | async-start | bytes 10948608 | tf_op jit(solution)/shard_map/all_gather | solution.py:470
  12.0 0.7 copy-start.22
  12.8 365.9 %reduce-scatter.2.cloned.1.call-start = ((), (), s32[]{:S(2)}) async-start(), calls=%async_computation.2 | async-start | bytes 10948608 | tf_op jit(solution)/shard_map/reduce_scatter | solution.py:474
  68.2 7.4 %copy-start = (bf16[2,2,512,768]{3,2,1,0:T(8,128)(2,1)S(1)}, bf16[2,2,512,768]{3,2,1,0:T(8,128)(2,1)}, u32[]{:S(2)}) copy-start(bf16[2,2,512,768]{3,2,1,0:T(8,128)(2,1)} %get-tuple-element.28) | copy-start | bytes 9437188
  76.7 1.5 copy-start.26
  78.2 5.9 %copy-start.25 = (s32[2,1,4]{2,1,0:T(1,128)S(1)}, s32[2,1,4]{2,1,0:T(1,128)}, u32[]{:S(2)}) copy-start(s32[2,1,4]{2,1,0:T(1,128)} %param.17) | copy-start | bytes 100
  84.1 34.8 %collective-permute-start = (bf16[512,768]{1,0:T(8,128)(2,1)}, bf16[512,768]{1,0:T(8,128)(2,1)}, u32[]{:S(2)}, u32[]{:S(2)}) collective-permute-start(bf16[512,768]{1,0:T(8,128)(2,1)} %dynamic-slice_bitcast_fusion.4), channel_id=1, source_target_pairs={{0,2},{1,3},{2,0},{3,1},{4,6},{5,7},{6,4},{7,5},{8,10},{9,11},{10,... | collective-permute-start | bytes 2359304 | tf_op jit(solution)/shard_map/ppermute | solution.py:586
  84.4 1.2 copy-start.23
  121.0 7.7 %collective-permute-start.1 = (bf16[2,512,384]{2,1,0:T(8,128)(2,1)}, bf16[2,512,384]{2,1,0:T(8,128)(2,1)}, u32[]{:S(2)}, u32[]{:S(2)}) collective-permute-start(bf16[2,512,384]{2,1,0:T(8,128)(2,1)} %dynamic-slice_bitcast_fusion.3), channel_id=1, source_target_pairs={{0,1},{1,0},{2,3},{3,2},{4,5},{5,4},{6,7},{7,6},{8,9},{9,8},{10,11... | collective-permute-start | bytes 2359304 | tf_op jit(solution)/shard_map/ppermute | solution.py:592
  123.5 2.0 copy-start.17
  125.5 3.2 copy-start.18
  127.0 3.0 copy-start.3
  127.0 3.0 copy-start.5
  136.5 17.3 %copy-start.10 = (bf16[32,96,768]{2,1,0:T(8,128)(2,1)}, bf16[32,96,768]{2,1,0:T(8,128)(2,1)S(1)}, u32[]{:S(2)}) copy-start(bf16[32,96,768]{2,1,0:T(8,128)(2,1)S(1)} %slice.238) | copy-start | bytes 14155780
  136.5 4.9 %copy-start.15 = (bf16[2,512,768]{2,1,0:T(8,128)(2,1)S(1)}, bf16[2,512,768]{2,1,0:T(8,128)(2,1)}, u32[]{:S(2)}) copy-start(bf16[2,512,768]{2,1,0:T(8,128)(2,1)} %pad_maximum_fusion.1) | copy-start | bytes 4718596
  136.5 5.3 %copy-start.20 = (bf16[2,1,512,768]{3,2,1,0:T(8,128)(2,1)S(1)}, bf16[2,1,512,768]{3,2,1,0:T(8,128)(2,1)}, u32[]{:S(2)}) copy-start(bf16[2,1,512,768]{3,2,1,0:T(8,128)(2,1)} %constant_dynamic-slice_fusion.3) | copy-start | bytes 4718596
  141.3 2.7 copy-start.21
  143.5 44.2 %copy-start.7 = (f32[1024,768]{1,0:T(8,128)}, f32[1024,768]{1,0:T(8,128)S(1)}, u32[]{:S(2)}) copy-start(f32[1024,768]{1,0:T(8,128)S(1)} %get-tuple-element.121) | copy-start | bytes 9437188
  144.0 9.8 %copy-start.16 = (bf16[2,512,768]{2,1,0:T(8,128)(2,1)S(1)}, bf16[2,512,768]{2,1,0:T(8,128)(2,1)}, u32[]{:S(2)}) copy-start(bf16[2,512,768]{2,1,0:T(8,128)(2,1)} %get-tuple-element.55) | copy-start | bytes 4718596
  187.7 1.5 copy-start.4
  187.7 1.5 copy-start.6
  189.2 1.7 copy-start.1
  205.2 8.4 %collective-permute-start.3 = (bf16[1024,384]{1,0:T(8,128)(2,1)S(1)}, bf16[1024,384]{1,0:T(8,128)(2,1)S(1)}, u32[]{:S(2)}, u32[]{:S(2)}) collective-permute-start(bf16[1024,384]{1,0:T(8,128)(2,1)S(1)} %constant_dynamic-slice_fusion), channel_id=1, source_target_pairs={{0,1},{1,0},{2,3},{3,2},{4,5},{5,4},{6,7},{7,6},{8,9},{9,8},{10,11... | collective-permute-start | bytes 2359304 | tf_op jit(solution)/shard_map/ppermute | solution.py:635
  231.6 1.1 copy-start.19
  233.7 65.2 %collective-permute-start.2 = (bf16[512,768]{1,0:T(8,128)(2,1)}, bf16[512,768]{1,0:T(8,128)(2,1)}, u32[]{:S(2)}, u32[]{:S(2)}) collective-permute-start(bf16[512,768]{1,0:T(8,128)(2,1)} %dynamic-slice_bitcast_fusion.2), channel_id=1, source_target_pairs={{0,2},{1,3},{2,0},{3,1},{4,6},{5,7},{6,4},{7,5},{8,10},{9,11},{10,... | collective-permute-start | bytes 2359304 | tf_op jit(solution)/shard_map/ppermute | solution.py:519
  288.6 9.2 %copy-start.11 = (bf16[2048,1152]{1,0:T(8,128)(2,1)S(1)}, bf16[2048,1152]{1,0:T(8,128)(2,1)}, u32[]{:S(2)}) copy-start(bf16[2048,1152]{1,0:T(8,128)(2,1)} %attend_backward.1) | copy-start | bytes 14155780
  296.0 2.6 copy-start.13
  297.4 12.8 %collective-permute-start.4 = (bf16[2,512,768]{2,1,0:T(8,128)(2,1)}, bf16[2,512,768]{2,1,0:T(8,128)(2,1)}, u32[]{:S(2)}, u32[]{:S(2)}) collective-permute-start(bf16[2,512,768]{2,1,0:T(8,128)(2,1)} %dynamic-slice_bitcast_fusion), channel_id=1, source_target_pairs={{0,1},{1,0},{2,3},{3,2},{4,5},{5,4},{6,7},{7,6},{8,9},{9,8},{10,11... | collective-permute-start | bytes 4718600 | tf_op jit(solution)/shard_map/ppermute | solution.py:644
  298.9 2.9 copy-start.12
  301.9 8.3 %copy-start.14 = (bf16[2048,768]{1,0:T(8,128)(2,1)S(1)}, bf16[2048,768]{1,0:T(8,128)(2,1)}, u32[]{:S(2)}) copy-start(bf16[2048,768]{1,0:T(8,128)(2,1)} %copy-done.13) | copy-start | bytes 9437188
  312.9 1.7 copy-start.2
  321.6 1.1 copy-start.8
  322.8 53.2 %copy-start.9 = (bf16[1024,768]{1,0:T(8,128)(2,1)S(1)}, bf16[1024,768]{1,0:T(8,128)(2,1)}, u32[]{:S(2)}) copy-start(bf16[1024,768]{1,0:T(8,128)(2,1)} %copy-done.8) | copy-start | bytes 4718596
  322.8 53.2 %collective-permute-start.5 = (bf16[512,768]{1,0:T(8,128)(2,1)S(1)}, bf16[512,768]{1,0:T(8,128)(2,1)}, u32[]{:S(2)}, u32[]{:S(2)}) collective-permute-start(bf16[512,768]{1,0:T(8,128)(2,1)S(1)} %dynamic-slice_bitcast_fusion.1), channel_id=1, source_target_pairs={{0,2},{1,3},{2,0},{3,1},{4,6},{5,7},{6,4},{7,5},{8,10},{9,11},{10,... | collective-permute-start | bytes 2359304 | tf_op jit(solution)/shard_map/ppermute | solution.py:519
  376.0 2.6 copy-start.24
Sparse Core Ops, SparseCore 0:
  12.9 120.8 all-gather.1
  215.4 146.4 reduce-scatter.1
